TPU v7x, 32 devices: a whole 2x2x4 slice. The times are simulated.
32 devices in a mesh: seq: 8 (over z, y), view: 4 (over x, core).
Axes of the slice: x: 2, y: 2, z: 4, core: 2. Of those that a mesh axis runs over, the one named last changes fastest.
Arguments:
- ssd_input: bfloat16 [8, 4, 512, 2048], P('seq', 'view'), may hold values from -21 to 21
- gate_input: bfloat16 [8, 4, 512, 2048], P('seq', 'view'), may hold values from -6 to 6
- b_matrix: bfloat16 [8, 4, 512, 128], P('seq', 'view'), may hold values from -6 to 6
- c_matrix: bfloat16 [8, 4, 512, 128], P('seq', 'view'), may hold values from -0.52734375 to 0.52734375
- log_decay: float32 [8, 4, 32, 512], P('seq', 'view'), may hold values from -1 to 0, as said below
- d_skip: float32 [32], replicated, may hold values from 1 to 4
- norm_gain: float32 [2048], replicated, may hold values from 0.1 to 1.9
- out_weight: bfloat16 [2048, 1536], replicated, may hold values from -0.125 to 0.125
- view_order: int32 [8, 4], P('seq'), may hold values from 0 to 3, each once within a row
- tile_order: int32 [8, 4], P('seq'), may hold values from 0 to 3, each once within a row
Outputs:
- next_tokens: bfloat16 [8, 4, 512, 1536], P('seq', 'view')
Inputs may be any that keep to these rules, and one draw needn't show every extreme that they name: `log_decay`: negative everywhere. `view_order`: each row is a permutation of the views. `tile_order`: each row is a permutation of the tiles of a block.
All inputs are finite; a program needn't handle non-finite values.
Results may differ from a plain program's by a relative error of at most 0.0059.
Values may be sent and summed in bfloat16 or wider, within the bound.
A program may use at most 128 MiB of HBM per device.

v0:
```python
import jax
import jax.numpy as jnp
from jax import lax
from jax.sharding import PartitionSpec as P

H = 32
HEAD = 64
N = 128
GROUP = 256
TILE = 128
TOKENS_PER_BLOCK = 512


EPS = 1e-05


def carried_in(x, axis, combine, identity):
    count, position = (lax.axis_size(axis), lax.axis_index(axis))
    everything = jax.tree.map(lambda part: lax.all_gather(part, axis), x)
    start = jax.tree.map(
        lambda part, zero: jnp.broadcast_to(jnp.asarray(zero, part.dtype), part.shape), x, identity
    )

    def hop(k, before):
        reached = k < position
        new = combine(before, jax.tree.map(lambda part: part[k], everything))
        return jax.tree.map(lambda a, b: jnp.where(reached, a, b), new, before)

    return lax.fori_loop(0, count, hop, start)


def compose(earlier, later):
    return (earlier[0] * later[0], later[0][:, None, None] * earlier[1] + later[1])


def masked_product(decays, keep_mask):
    return jnp.prod(jnp.where(keep_mask[:, :, None], decays[None], 1.0), axis=1)


def shards(
    ssd_input,
    gate_input,
    b_matrix,
    c_matrix,
    log_decay,
    d_skip,
    norm_gain,
    out_weight,
    view_order,
    tile_order,
):
    group_count = TOKENS_PER_BLOCK // GROUP
    view_count = lax.axis_size("view")
    band_count = lax.axis_size("seq")
    piece_len = TOKENS_PER_BLOCK // band_count
    x_groups = ssd_input[0, 0].reshape(group_count, GROUP, H, HEAD)
    b_groups = b_matrix[0, 0].reshape(group_count, GROUP, N)
    c_groups = c_matrix[0, 0].reshape(group_count, GROUP, N)
    cum_log = jnp.cumsum(log_decay[0, 0].reshape(H, group_count, GROUP), axis=2)
    group_end = cum_log[:, :, GROUP - 1]
    group_decay = jnp.exp(group_end)
    scaled = (
        jnp.exp(group_end[:, :, None] - cum_log)[..., None] * b_groups[None].astype(jnp.float32)
    ).astype(jnp.bfloat16)
    states = jnp.einsum("hckn,ckhp->hcpn", scaled, x_groups, preferred_element_type=jnp.float32)
    running = jnp.zeros((H, HEAD, N), jnp.float32)
    before = jnp.ones((H,), jnp.float32)
    prefixes = []
    befores = []
    for lookup_index in range(group_count):
        prefixes.append(running)
        befores.append(before)
        running = group_decay[:, lookup_index, None, None] * running + states[:, lookup_index]
        before = before * group_decay[:, lookup_index]
    band_order = view_order[0]
    view_slots = jnp.arange(view_count, dtype=jnp.int32)
    order_hot = band_order[:, None] == view_slots[None, :]
    view_rank = jnp.sum(jnp.where(order_hot, view_slots[:, None], 0), axis=0)
    my_view = lax.axis_index("view")
    heads_share = H // view_count
    all_decay = lax.all_gather(before[None], "view", axis=0, tiled=True)
    share_decay = lax.dynamic_slice_in_dim(all_decay, my_view * heads_share, heads_share, 1)
    split_state = running.reshape(view_count, heads_share, HEAD, N)
    view_states = lax.all_to_all(split_state, "view", split_axis=0, concat_axis=0, tiled=True)
    after_mask = view_rank[None, :] > view_rank[:, None]
    to_total = masked_product(share_decay, after_mask)
    share_state = jnp.sum(to_total[:, :, None, None] * view_states, axis=0)
    share_row_decay = jnp.prod(share_decay, axis=0)
    identity = (jnp.ones_like(share_row_decay), jnp.zeros_like(share_state))
    _, share_in = carried_in((share_row_decay, share_state), "seq", compose, identity)
    pre_decays = masked_product(share_decay, view_rank[None, :] < view_rank[:, None])
    targets = []
    for target in range(view_count):
        target_rank = view_rank[target]
        between = after_mask & (view_rank[None, :] < target_rank)
        to_target = jnp.where(
            (view_rank < target_rank)[:, None], masked_product(share_decay, between), 0.0
        )
        within = jnp.sum(to_target[:, :, None, None] * view_states, axis=0)
        targets.append(pre_decays[target][:, None, None] * share_in + within)
    target_states = jnp.stack(targets, axis=0)
    entering = lax.all_to_all(target_states, "view", split_axis=0, concat_axis=1, tiled=True)[0]
    entries = jnp.stack(
        [prefix + factor[:, None, None] * entering for prefix, factor in zip(prefixes, befores)],
        axis=1,
    ).astype(jnp.bfloat16)
    scores = jnp.einsum("cqn,ckn->cqk", c_groups, b_groups, preferred_element_type=jnp.float32)
    log_gaps = cum_log[:, :, :, None] - cum_log[:, :, None, :]
    causal = jnp.tril(jnp.ones((GROUP, GROUP), dtype=bool))
    weights = (jnp.exp(jnp.where(causal, log_gaps, -jnp.inf)) * scores[None]).astype(jnp.bfloat16)
    inside = jnp.einsum("hcqk,ckhp->cqhp", weights, x_groups, preferred_element_type=jnp.float32)
    carried = jnp.einsum("cqn,hcpn->cqhp", c_groups, entries, preferred_element_type=jnp.float32)
    carried = carried * jnp.transpose(jnp.exp(cum_log), (1, 2, 0))[..., None]
    mixed = inside + carried + d_skip[None, None, :, None] * x_groups.astype(jnp.float32)
    gated = mixed * jax.nn.silu(
        gate_input[0, 0].reshape(group_count, GROUP, H, HEAD).astype(jnp.float32)
    )
    inv_rms = lax.rsqrt(jnp.mean(gated * gated, axis=-1, keepdims=True) + EPS)
    normed = (
        (gated * inv_rms * norm_gain.reshape(H, HEAD))
        .astype(jnp.bfloat16)
        .reshape(band_count, piece_len, H * HEAD)
    )
    arrived = jnp.einsum(
        "bpd,de->bpe",
        lax.all_to_all(normed, "seq", split_axis=0, concat_axis=0, tiled=True),
        out_weight,
        preferred_element_type=jnp.float32,
    ).astype(jnp.bfloat16)
    width_out = out_weight.shape[1]
    tile_rows = arrived.reshape(TOKENS_PER_BLOCK // TILE, TILE, width_out)
    chosen = jnp.take(tile_rows, tile_order[0], axis=0)
    return chosen.reshape(1, 1, TOKENS_PER_BLOCK, width_out)


def solution(mesh):
    in_specs = (
        P("seq", "view", None, None),
        P("seq", "view", None, None),
        P("seq", "view", None, None),
        P("seq", "view", None, None),
        P("seq", "view", None, None),
        P(),
        P(),
        P(),
        P("seq", None),
        P("seq", None),
    )
    out_specs = P("seq", "view", None, None)
    return jax.shard_map(shards, mesh=mesh, in_specs=in_specs, out_specs=out_specs, check_vma=False)
```

profile of v0, /device:TPU:0, one launch (start us, length us, event | category | flops | bytes accessed | tf_op | source)
XLA Modules:
  0.0 224.0 jit_solution(10633547949898538085)
XLA Ops:
  9.9 2.9 %copy.66 = bf16[1,1,512,2048]{2,3,1,0:T(8,128)(2,1)S(1)} copy(bf16[1,1,512,2048]{3,2,1,0:T(8,128)(2,1)} %param.12) | data formatting | bytes 4194304 | tf_op args[0]
  12.8 2.1 reshape_squeeze.13
  15.7 4.6 %fusion.20 = f32[32,2,64,128]{3,2,1,0:T(8,128)S(1)} fusion(f32[2,256,128]{2,1,0:T(8,128)S(1)} %convert_element_type.31, f32[32,2,256]{2,1,0:T(2,128)S(1)} %copy.68, bf16[2,256,32,64]{1,0,3,2:T(2,128)(2,1)} %reshape_squeeze.13), kind=kOutput, calls=%fused_computation.26 | convolution fusion | flops 272629760 | bytes 4521984 | tf_op jit(solution)/shard_map/hckn,ckhp->hcpn/dot_general | solution.py:65
  20.6 1.2 bitcast_add_fusion.1
  21.7 4.2 %all-to-all-start = ((f32[4,8,64,128]{3,2,1,0:T(8,128)}), f32[4,8,64,128]{3,2,1,0:T(8,128)S(1)}, u32[]{:S(2)}, u32[]{:S(2)}) async-start(f32[4,8,64,128]{3,2,1,0:T(8,128)} %bitcast_add_fusion.1), calls=%async_computation | async-start | bytes 2097152 | tf_op jit(solution)/shard_map/all_to_all | solution.py:84
  28.0 13.8 %all-reduce.2 = f32[4,32]{1,0:T(4,128)S(1)} all-reduce(f32[4,32]{1,0:T(4,128)S(1)} %reshape.489), channel_id=2, replica_groups=mesh['seq'=8,'view'=4] {'view'}, use_global_device_ids=true, to_apply=%add | all-reduce | flops 128 | bytes 1024
  43.2 2.5 %broadcast_compare_fusion.2 = (pred[4]{0:T(512)(128)(4,1)S(1)}, pred[4]{0:T(512)(128)(4,1)S(1)}, pred[4]{0:T(512)(128)(4,1)S(1)}, pred[4]{0:T(512)(128)(4,1)S(1)}) fusion(s32[4]{0:T(128)S(1)} %select_reduce_fusion.6, s32[]{:T(128)} %bitcast.24, s32[]{:T(128)} %bitcast.21, s32[]{:T(128)} %bitcast.18, s32[]{:T(128)} %bitcast.15), kind=kLoop, calls=%fused_computation.84 | loop fusion | flops 16 | bytes 48 | tf_op jit(solution)/shard_map/lt | solution.py:97
  46.7 2.2 multiply_reduce_fusion.4
  48.9 1.4 dynamic-slice.1
  51.7 22.5 %all-reduce.1 = f32[64]{0:T(128)S(1)} all-reduce(f32[64]{0:T(128)S(1)} %dynamic-update-slice.1), channel_id=3, replica_groups=mesh['seq'=8,'view'=4] {'seq'}, use_global_device_ids=true, to_apply=%add.1 | all-reduce | flops 64 | bytes 512
  74.9 25.7 %all-gather.5.cloned.1.call-done = f32[64,64,128]{2,1,0:T(8,128)} async-done(((f32[8,64,128]{2,1,0:T(8,128)}), f32[64,64,128]{2,1,0:T(8,128)}) %all-gather.5.cloned.1.call-update) | async-done | bytes 2097168 | tf_op jit(solution)/shard_map/all_gather | solution.py:19
  100.6 8.7 %while.14 = (s32[]{:T(128)}, f32[8,64,128]{2,1,0:T(8,128)S(1)}, s32[]{:T(128)}, f32[8,8]{1,0:T(8,128)S(1)}, f32[8,8,64,128]{3,2,1,0:T(8,128)}, /*index=5*/s32[]{:T(128)}, s32[]{:T(128)}) while((s32[]{:T(128)}, f32[8,64,128]{2,1,0:T(8,128)S(1)}, s32[]{:T(128)}, f32[8,8]{1,0:T(8,128)S(1)}, f32[8,8,64,128]{3,2,1,0:T(8,128)}, ...), condition=%wide.region_8.9_spmd.clone, body=%wide.region_7.8_spmd.clone.sunk | while | flops 262148 | bytes 786641 | solution.py:29
  111.2 3.7 %all-to-all-start.1 = ((f32[4,8,64,128]{3,2,1,0:T(8,128)}), f32[4,8,64,128]{3,2,1,0:T(8,128)S(1)}, u32[]{:S(2)}, u32[]{:S(2)}) async-start(f32[4,8,64,128]{3,2,1,0:T(8,128)} %pad_maximum_fusion), calls=%async_computation.1 | async-start | bytes 2097152 | tf_op jit(solution)/shard_map/all_to_all | solution.py:102
  114.9 7.4 %reshape.505 = f32[2,256,32,64]{3,2,1,0:T(8,128)} reshape(bf16[1,1,512,2048]{3,2,1,0:T(8,128)(2,1)} %param.13) | data formatting | bytes 6291456 | tf_op jit(solution)/shard_map/convert_element_type | solution.py:116
  122.3 7.9 %copy.74 = f32[2,256,32,64]{1,3,2,0:T(8,128)} copy(f32[2,256,32,64]{3,2,1,0:T(8,128)} %reshape.505) | data formatting | bytes 8388608 | tf_op jit(solution)/shard_map/convert_element_type | solution.py:116
  132.4 1.2 copy-done.1
  134.3 5.6 %multiply_reduce_fusion = (f32[2,256,32]{1,2,0:T(8,128)S(1)}, f32[2,256,32,64]{1,3,2,0:T(8,128)S(1)}) fusion(f32[2,256,32,64]{1,3,2,0:T(8,128)S(1)} %copy-done.1, bf16[2,256,32,64]{1,0,3,2:T(2,128)(2,1)S(1)} %copy-done.2, f32[32]{0:T(128)S(1)} %copy-done.16, f32[2,256,32]{1,2,0:T(8,128)S(1)} %copy-done.11, f32[2,32,64,256]{3,2,1,0:T(8,128)S(1)} %fusion.24, ...), kind=kOutput, calls=%fused_computation.20 | convolution fusion | flops 566214656 | bytes 15466624 | tf_op jit(solution)/shard_map/hcqk,ckhp->cqhp/dot_general | solution.py:111
  140.5 6.6 %copy.75 = bf16[2,256,32,64]{3,2,1,0:T(8,128)(2,1)} copy(bf16[2,256,32,64]{1,3,2,0:T(8,128)(2,1)S(1)} %multiply_convert_fusion.4) | data formatting | bytes 4194304 | tf_op jit(solution)/shard_map/convert_element_type | solution.py:121
  147.2 6.8 %reshape.478 = bf16[8,64,2048]{2,1,0:T(8,128)(2,1)} reshape(bf16[2,256,32,64]{3,2,1,0:T(8,128)(2,1)} %copy.75) | data formatting | bytes 4194304 | tf_op jit(solution)/shard_map/reshape | solution.py:122
  154.0 3.6 %all-to-all-start.2 = ((bf16[8,64,2048]{2,1,0:T(8,128)(2,1)}), bf16[8,64,2048]{2,1,0:T(8,128)(2,1)S(1)}, u32[]{:S(2)}, u32[]{:S(2)}) async-start(bf16[8,64,2048]{2,1,0:T(8,128)(2,1)} %reshape.478), calls=%async_computation.2 | async-start | bytes 4194304 | tf_op jit(solution)/shard_map/all_to_all | solution.py:126
  157.7 48.8 %all-to-all-done.2 = bf16[8,64,2048]{2,1,0:T(8,128)(2,1)S(1)} async-done(((bf16[8,64,2048]{2,1,0:T(8,128)(2,1)}), bf16[8,64,2048]{2,1,0:T(8,128)(2,1)S(1)}, u32[]{:S(2)}, u32[]{:S(2)}) %all-to-all-start.2) | async-done | bytes 2097184 | tf_op jit(solution)/shard_map/all_to_all | solution.py:126
  206.4 7.3 %fusion.15 = bf16[8,64,1536]{2,1,0:T(8,128)(2,1)} fusion(bf16[8,64,2048]{2,1,0:T(8,128)(2,1)S(1)} %all-to-all-done.2, bf16[2048,1536]{1,0:T(8,128)(2,1)} %param.19), kind=kOutput, calls=%fused_computation.23 | convolution fusion | flops 3222011904 | bytes 9961472 | tf_op jit(solution)/shard_map/bpd,de->bpe/dot_general | solution.py:124
  213.7 2.1 gather_fusion
  215.8 1.4 broadcast_select_fusion
  (105 shorter events, 23.4 us)
Async XLA Ops:
  6.5 123.8 %copy-start = (bf16[1,1,512,128]{3,2,1,0:T(8,128)(2,1)S(1)}, bf16[1,1,512,128]{3,2,1,0:T(8,128)(2,1)}, u32[]{:S(2)}) copy-start(bf16[1,1,512,128]{3,2,1,0:T(8,128)(2,1)} %param.15) | copy-start | bytes 393220
  9.0 0.9 copy-start.9
  9.9 5.7 %copy-start.7 = (bf16[1,1,512,128]{3,2,1,0:T(8,128)(2,1)S(1)}, bf16[1,1,512,128]{3,2,1,0:T(8,128)(2,1)}, u32[]{:S(2)}) copy-start(bf16[1,1,512,128]{3,2,1,0:T(8,128)(2,1)} %param.14) | copy-start | bytes 393220
  20.3 5.7 %copy-start.18 = (u32[32]{0:T(128)S(1)}, u32[32]{0:T(128)}, u32[]{:S(2)}) copy-start(u32[32]{0:T(128)} %constant.82) | copy-start | bytes 388
  20.3 21.6 %copy-start.15 = (s32[1,4]{1,0:T(1,128)S(1)}, s32[1,4]{1,0:T(1,128)}, u32[]{:S(2)}) copy-start(s32[1,4]{1,0:T(1,128)} %param.20) | copy-start | bytes 52
  21.7 25.0 %all-to-all-start = ((f32[4,8,64,128]{3,2,1,0:T(8,128)}), f32[4,8,64,128]{3,2,1,0:T(8,128)S(1)}, u32[]{:S(2)}, u32[]{:S(2)}) async-start(f32[4,8,64,128]{3,2,1,0:T(8,128)} %bitcast_add_fusion.1), calls=%async_computation | async-start | bytes 2097152 | tf_op jit(solution)/shard_map/all_to_all | solution.py:84
  26.0 74.6 %all-gather.5.cloned.1.call-start = ((), (), s32[]{:S(2)}) async-start(), calls=%async_computation.3 | async-start | bytes 2359296 | tf_op jit(solution)/shard_map/all_gather | solution.py:19
  48.9 60.5 %copy-start.3 = (f32[8,64,128]{2,1,0:T(8,128)S(1)}, f32[8,64,128]{2,1,0:T(8,128)}, u32[]{:S(2)}) copy-start(f32[8,64,128]{2,1,0:T(8,128)} %get-tuple-element.119) | copy-start | bytes 786436
  48.9 60.5 %copy-start.4 = (f32[8,64,128]{2,1,0:T(8,128)S(1)}, f32[8,64,128]{2,1,0:T(8,128)}, u32[]{:S(2)}) copy-start(f32[8,64,128]{2,1,0:T(8,128)} %get-tuple-element.120) | copy-start | bytes 786436
  48.9 60.5 %copy-start.5 = (f32[8,64,128]{2,1,0:T(8,128)S(1)}, f32[8,64,128]{2,1,0:T(8,128)}, u32[]{:S(2)}) copy-start(f32[8,64,128]{2,1,0:T(8,128)} %get-tuple-element.121) | copy-start | bytes 786436
  111.2 20.1 %all-to-all-start.1 = ((f32[4,8,64,128]{3,2,1,0:T(8,128)}), f32[4,8,64,128]{3,2,1,0:T(8,128)S(1)}, u32[]{:S(2)}, u32[]{:S(2)}) async-start(f32[4,8,64,128]{3,2,1,0:T(8,128)} %pad_maximum_fusion), calls=%async_computation.1 | async-start | bytes 2097152 | tf_op jit(solution)/shard_map/all_to_all | solution.py:102
  122.3 7.9 %copy-start.12 = (f32[2048]{0:T(1024)S(1)}, f32[2048]{0:T(1024)}, u32[]{:S(2)}) copy-start(f32[2048]{0:T(1024)} %param.18) | copy-start | bytes 24580
  122.3 8.0 %copy-start.8 = (bf16[1,1,512,128]{3,2,1,0:T(8,128)(2,1)S(1)}, bf16[1,1,512,128]{3,2,1,0:T(8,128)(2,1)}, u32[]{:S(2)}) copy-start(bf16[1,1,512,128]{3,2,1,0:T(8,128)(2,1)} %param.14) | copy-start | bytes 393220
  122.3 9.2 %copy-start.13 = (f32[32]{0:T(128)S(1)}, f32[32]{0:T(128)}, u32[]{:S(2)}) copy-start(f32[32]{0:T(128)} %get-tuple-element.157) | copy-start | bytes 388
  122.3 9.2 %copy-start.14 = (f32[32]{0:T(128)S(1)}, f32[32]{0:T(128)}, u32[]{:S(2)}) copy-start(f32[32]{0:T(128)} %get-tuple-element.155) | copy-start | bytes 388
  131.4 2.2 copy-start.1
  131.4 2.9 %copy-start.2 = (bf16[2,256,32,64]{1,0,3,2:T(2,128)(2,1)S(1)}, bf16[2,256,32,64]{1,0,3,2:T(2,128)(2,1)}, u32[]{:S(2)}) copy-start(bf16[2,256,32,64]{1,0,3,2:T(2,128)(2,1)} %reshape_squeeze.13) | copy-start | bytes 6291460
  131.4 2.9 %copy-start.6 = (f32[2,256,256]{2,1,0:T(8,128)S(1)}, f32[2,256,256]{2,1,0:T(8,128)}, u32[]{:S(2)}) copy-start(f32[2,256,256]{2,1,0:T(8,128)} %fusion.31) | copy-start | bytes 1572868
  131.5 2.9 %copy-start.10 = (f32[32,2,256]{2,0,1:T(8,128)S(1)}, f32[32,2,256]{2,0,1:T(8,128)}, u32[]{:S(2)}) copy-start(f32[32,2,256]{2,0,1:T(8,128)} %copy-done.9) | copy-start | bytes 196612
  131.5 2.9 %copy-start.11 = (f32[2,256,32]{1,2,0:T(8,128)S(1)}, f32[2,256,32]{1,2,0:T(8,128)}, u32[]{:S(2)}) copy-start(f32[2,256,32]{1,2,0:T(8,128)} %get-tuple-element.149) | copy-start | bytes 196612
  131.5 2.9 %copy-start.16 = (f32[32]{0:T(128)S(1)}, f32[32]{0:T(128)}, u32[]{:S(2)}) copy-start(f32[32]{0:T(128)} %param.17) | copy-start | bytes 388
  147.2 10.4 %copy-start.17 = (s32[1,4]{1,0:T(1,128)S(1)}, s32[1,4]{1,0:T(1,128)}, u32[]{:S(2)}) copy-start(s32[1,4]{1,0:T(1,128)} %param.21) | copy-start | bytes 52
  154.0 52.5 %all-to-all-start.2 = ((bf16[8,64,2048]{2,1,0:T(8,128)(2,1)}), bf16[8,64,2048]{2,1,0:T(8,128)(2,1)S(1)}, u32[]{:S(2)}, u32[]{:S(2)}) async-start(bf16[8,64,2048]{2,1,0:T(8,128)(2,1)} %reshape.478), calls=%async_computation.2 | async-start | bytes 4194304 | tf_op jit(solution)/shard_map/all_to_all | solution.py:126
Sparse Core Ops, SparseCore 0:
  49.0 51.5 all-gather.4
where the time goes:
time: 225 us; the launch traced here: 224 us
  waiting for transfers between devices  74.5 us (33%)
  local copies, waits for them, and re-layouts  43.9 us (20%)
  blocking collectives  36.3 us (16%)
  other arithmetic  23.2 us (10%)
  matrix products  19.1 us (8%)
  between operations  15.1 us (7%)
  starting transfers between devices  11.5 us (5%)
    all_to_all x1, waiting for transfers between devices, shards(): lax.all_to_all(normed, 'seq', split_axis=0, concat_axis=0, tiled=True)  48.8 us
    unnamed x2, blocking collectives  36.3 us
    all_gather x1, waiting for transfers between devices, carried_in(): everything = jax.tree.map(lambda part: lax.all_gather(part, axis), x)  25.7 us
    convert_element_type x2, local copies, waits for them, and re-layouts, shards(): gate_input[0, 0].reshape(group_count, GROUP, H, HEAD).astype(jnp.float32)  15.2 us
    select_n x8, other arithmetic, hop(): return jax.tree.map(lambda a, b: jnp.where(reached, a, b), new, before)  8.42 us
    unnamed x44, local copies, waits for them, and re-layouts  7.7 us
    dot_general x1, matrix products, shards(): jnp.einsum('bpd,de->bpe', lax.all_to_all(normed, 'seq', split_axis=0, con...  7.25 us
    reshape x1, local copies, waits for them, and re-layouts, shards(): normed = (gated * inv_rms * norm_gain.reshape(H, HEAD)).astype(jnp.bfloat...  6.77 us
  transfers between devices with their start and end apart: 4, of which 2 were waited for; matrix products, arithmetic and copies ran while one was open for 11% of the time, Pallas kernels for 0%

commit v1 on v0

v1 whole, which is shorter than its diff:
```python
import functools

import jax
import jax.numpy as jnp
from jax import lax
from jax.experimental import pallas as pl
from jax.experimental.pallas import tpu as pltpu
from jax.sharding import PartitionSpec as P

GROUP = 256
TILE = 128
EPS = 1e-05
MESH = pl.DeviceIdType.MESH
F32 = jnp.float32
BF16 = jnp.bfloat16
VMEM = pltpu.VMEM


def nn(a, b):
    return lax.dot_general(a, b, (((1,), (0,)), ((), ())), preferred_element_type=F32)


def nt(a, b):
    return lax.dot_general(a, b, (((1,), (1,)), ((), ())), preferred_element_type=F32)


def tn(a, b):
    return lax.dot_general(a, b, (((0,), (0,)), ((), ())), preferred_element_type=F32)


def split3(a):
    hi = a.astype(BF16)
    rest = a - hi.astype(F32)
    mid = rest.astype(BF16)
    low = (rest - mid.astype(F32)).astype(BF16)
    return hi, mid, low


def iota(shape, dim):
    return lax.broadcasted_iota(jnp.int32, shape, dim)


def pair_columns(full, pair):
    lanes = full.shape[1]
    turned = pltpu.roll(full, lax.rem(lanes - 2 * pair, lanes), 1)
    return turned[:, 0:1], turned[:, 1:2]


def local_kernel(
    x_ref, b_ref, c_ref, ld_ref, skip_ref,
    inside_ref, state_ref, prefix_ref, ecol_ref, total_ref,
    row_s, col_s, score_s,
):
    pair = pl.program_id(0)
    heads, tokens = ld_ref.shape
    groups = tokens // GROUP

    @pl.when(pair == 0)
    def _():
        at_row, at_col = iota((GROUP, GROUP), 0), iota((GROUP, GROUP), 1)
        lower = jnp.where(at_col <= at_row, 1.0, 0.0).astype(BF16)
        upper = jnp.where(at_row <= at_col, 1.0, 0.0).astype(BF16)
        total = jnp.zeros((heads, 1), F32)
        for c in range(groups):
            span = slice(c * GROUP, (c + 1) * GROUP)
            own = ld_ref[:, span]
            padded = jnp.concatenate([own, jnp.zeros((128 - heads, GROUP), F32)], axis=0)
            rows = sum(nn(part, upper) for part in split3(own))
            row_s[:, span] = rows
            cols = sum(nt(lower, part) for part in split3(padded))
            col_s[span, :] = cols
            ecol_ref[span, :] = jnp.exp(cols)
            total = total + rows[:, GROUP - 1 : GROUP]
            scores = nt(c_ref[span, :], b_ref[span, :])
            score_s[c] = jnp.where(at_col <= at_row, scores, 0.0)
        total_ref[...] = jnp.broadcast_to(total, total_ref.shape)

    first_half = iota((GROUP, 128), 1) < 64
    top_half = iota((128, 128), 0) < 64
    col0, col1 = pair_columns(col_s[...], pair)
    running = jnp.zeros((128, 128), F32)
    for c in range(groups):
        span = slice(c * GROUP, (c + 1) * GROUP)
        x = x_ref[span, :]
        xf = x.astype(F32)
        outs = []
        ends = []
        for j, col in enumerate((col0, col1)):
            row = row_s[pl.ds(2 * pair + j, 1), span]
            mine = col[span, :]
            gap = jnp.minimum(mine - row, 0.0)
            weights = (jnp.exp(gap) * score_s[c]).astype(BF16)
            outs.append(nn(weights, x))
            ends.append(mine[GROUP - 1 : GROUP, :])
        inside_ref[span, :] = jnp.where(first_half, outs[0], outs[1]) + skip_ref[...] * xf
        factor = jnp.where(first_half, ends[0] - col0[span, :], ends[1] - col1[span, :])
        scaled = (xf * jnp.exp(jnp.minimum(factor, 0.0))).astype(BF16)
        state = tn(scaled, b_ref[span, :])
        if c:
            prefix_ref[c - 1] = running
        decay = jnp.exp(jnp.where(top_half, ends[0], ends[1]))
        running = decay * running + state
    state_ref[...] = running.astype(BF16)


def local_part(x, b, c, ld, skip):
    tokens, width = x.shape
    heads = ld.shape[0]
    groups = tokens // GROUP
    pairs = width // 128
    whole = lambda shape: pl.BlockSpec(shape, lambda p: (0,) * len(shape))
    lanes = lambda rows: pl.BlockSpec((rows, 128), lambda p: (0, p))
    return pl.pallas_call(
        local_kernel,
        grid=(pairs,),
        in_specs=[lanes(tokens), whole(b.shape), whole(c.shape), whole(ld.shape), lanes(1)],
        out_specs=[
            lanes(tokens),
            pl.BlockSpec((128, 128), lambda p: (p, 0)),
            pl.BlockSpec((groups - 1, 128, 128), lambda p: (0, p, 0)),
            whole((tokens, 128)),
            whole((heads, 128)),
        ],
        out_shape=[
            jax.ShapeDtypeStruct((tokens, width), F32),
            jax.ShapeDtypeStruct((width, 128), BF16),
            jax.ShapeDtypeStruct((groups - 1, width, 128), F32),
            jax.ShapeDtypeStruct((tokens, 128), F32),
            jax.ShapeDtypeStruct((heads, 128), F32),
        ],
        scratch_shapes=[
            VMEM((heads, tokens), F32),
            VMEM((tokens, 128), F32),
            VMEM((groups, GROUP, GROUP), F32),
        ],
        name="local_part",
    )(x, b, c, ld, skip)


def scan_kernel(
    views, pack, groups, share,
    order_ref, state_ref, total_ref, out_ref,
    note_s, got_s, gotnote_s, agg_s, aggnote_s, aggs_s, aggnotes_s, within_s, before_s, send_s,
    sem_a, sem_an, sem_b, sem_bn, sem_c,
):
    band, view = lax.axis_index("seq"), lax.axis_index("view")
    count = views * pack
    group, member = band // pack, lax.rem(band, pack)
    me = member * views + view
    rows = share * 64

    def peer(q):
        return {"seq": group * pack + q // views, "view": lax.rem(q, views)}

    def across(g):
        return {"seq": g * pack + member, "view": view}

    barrier = pltpu.get_barrier_semaphore()
    for d in range(1, count):
        pl.semaphore_signal(
            barrier, inc=1, device_id=peer(lax.rem(me + d, count)), device_id_type=MESH
        )
    for d in range(1, groups):
        pl.semaphore_signal(
            barrier, inc=1, device_id=across(lax.rem(group + d, groups)), device_id_type=MESH
        )
    rank = jnp.int32(0)
    for r in range(views):
        rank = rank + jnp.where(order_ref[0, r] == view, r, 0)
    key = (rank + member * views).astype(F32)
    for q in range(count):
        note_s[q, 0:share, :] = total_ref[q * share : (q + 1) * share, :]
        note_s[q, share : share + 1, :] = jnp.full((1, 128), key, F32)
    pl.semaphore_wait(barrier, count - 1 + groups - 1)

    def exchange(source, target, sem, d, q):
        return pltpu.make_async_remote_copy(
            src_ref=source, dst_ref=target, send_sem=sem.at[0, d], recv_sem=sem.at[1, d],
            device_id=peer(q), device_id_type=MESH,
        )

    sends = []
    for d in range(1, count):
        q = lax.rem(me + d, count)
        sends.append(exchange(note_s.at[q], gotnote_s.at[me], sem_an, d, q))
        sends[-1].start()
        sends.append(exchange(state_ref.at[q], got_s.at[me], sem_a, d, q))
        sends[-1].start()
    got_s[me] = state_ref[me]
    gotnote_s[me] = note_s[me]
    for d in range(1, count):
        src = lax.rem(me - d + count, count)
        exchange(note_s.at[src], gotnote_s.at[src], sem_an, d, src).wait_recv()
        exchange(state_ref.at[src], got_s.at[src], sem_a, d, src).wait_recv()

    logs = [gotnote_s[b] for b in range(count)]
    keys = [jnp.broadcast_to(log[share : share + 1, :], log.shape) for log in logs]
    zero = jnp.zeros_like(logs[0])
    before, upto, whole = [], [], zero
    for b in range(count):
        acc = zero
        for o in range(count):
            if o != b:
                acc = acc + jnp.where(keys[o] < keys[b], logs[o], 0.0)
        before.append(acc)
        upto.append(acc + logs[b])
        before_s[b] = jnp.exp(acc)
        whole = whole + logs[b]
    aggnote_s[...] = whole
    last = [jnp.exp(jnp.minimum(whole - upto[b], 0.0)) for b in range(count)]
    for i in range(share):
        span = slice(i * 64, (i + 1) * 64)
        acc = jnp.zeros((64, 128), F32)
        for b in range(count):
            acc = acc + last[b][i : i + 1, :] * got_s[b, span, :].astype(F32)
        agg_s[span, :] = acc.astype(BF16)

    def ahead(source, target, sem, k, g):
        return pltpu.make_async_remote_copy(
            src_ref=source, dst_ref=target, send_sem=sem.at[0, k], recv_sem=sem.at[1, k],
            device_id=across(g), device_id_type=MESH,
        )

    def ahead_pair(k, g):
        return (
            ahead(aggnote_s, aggnotes_s.at[k], sem_bn, k, g),
            ahead(agg_s, aggs_s.at[k], sem_b, k, g),
        )

    for k in range(groups - 1, 0, -1):
        @pl.when(group + k < groups)
        def _(k=k):
            for copy in ahead_pair(k, group + k):
                copy.start()

    for b in range(count):
        coefs = [
            jnp.where(
                keys[o] < keys[b], jnp.exp(jnp.minimum(before[b] - upto[o], 0.0)), 0.0
            )
            for o in range(count)
            if o != b
        ]
        others = [o for o in range(count) if o != b]
        for i in range(share):
            span = slice(i * 64, (i + 1) * 64)
            acc = jnp.zeros((64, 128), F32)
            for o, coef in zip(others, coefs):
                acc = acc + coef[i : i + 1, :] * got_s[o, span, :].astype(F32)
            within_s[b, span, :] = acc

    carry = within_s.at[count]
    carry[...] = jnp.zeros((rows, 128), F32)
    for k in range(groups - 1, 0, -1):
        @pl.when(group - k >= 0)
        def _(k=k):
            for copy in ahead_pair(k, group - k):
                copy.wait_recv()
            decay = jnp.exp(aggnotes_s[k])
            for i in range(share):
                span = slice(i * 64, (i + 1) * 64)
                carry[span, :] = decay[i : i + 1, :] * carry[span, :] + aggs_s[k, span, :].astype(F32)

    def entering(q):
        factor = before_s[q]
        parts = []
        for i in range(share):
            span = slice(i * 64, (i + 1) * 64)
            parts.append(factor[i : i + 1, :] * carry[span, :] + within_s[q, span, :])
        return jnp.concatenate(parts, axis=0).astype(BF16)

    for d in range(1, count):
        q = lax.rem(me + d, count)
        send_s[d] = entering(q)
        sends.append(exchange(send_s.at[d], out_ref.at[me], sem_c, d, q))
        sends[-1].start()
    out_ref[me] = entering(me)
    for d in range(1, count):
        src = lax.rem(me - d + count, count)
        exchange(send_s.at[d], out_ref.at[src], sem_c, d, src).wait_recv()
    for copy in sends:
        copy.wait_send()
    for k in range(1, groups):
        @pl.when(group + k < groups)
        def _(k=k):
            for copy in ahead_pair(k, group + k):
                copy.wait_send()


def scan_part(order, state, total, views, bands):
    heads = total.shape[0]
    pack = 2 if bands % 2 == 0 and heads % (2 * views) == 0 else 1
    count = views * pack
    share = heads // count
    groups = bands // pack
    rows = share * 64
    vmem = pl.BlockSpec(memory_space=pltpu.VMEM)
    sems = lambda n: pltpu.SemaphoreType.DMA((2, n))
    return pl.pallas_call(
        functools.partial(scan_kernel, views, pack, groups, share),
        in_specs=[pl.BlockSpec(memory_space=pltpu.SMEM), vmem, vmem],
        out_specs=vmem,
        out_shape=jax.ShapeDtypeStruct((count, rows, 128), BF16),
        scratch_shapes=[
            VMEM((count, 8, 128), F32),
            VMEM((count, rows, 128), BF16),
            VMEM((count, 8, 128), F32),
            VMEM((rows, 128), BF16),
            VMEM((8, 128), F32),
            VMEM((groups, rows, 128), BF16),
            VMEM((groups, 8, 128), F32),
            VMEM((count + 1, rows, 128), F32),
            VMEM((count, 8, 128), F32),
            VMEM((count, rows, 128), BF16),
            sems(count), sems(count), sems(groups), sems(groups), sems(count),
        ],
        compiler_params=pltpu.CompilerParams(collective_id=0, has_side_effects=True),
        name="scan_part",
    )(order, state.reshape(count, rows, 128), total)


def token_kernel(
    inside_ref, gate_ref, ent_ref, prefix_ref, ecol_ref, c_ref, gain_ref, w_hbm, out_ref,
    normed_s, w_s, sem,
):
    pair = pl.program_id(0)
    tokens = inside_ref.shape[0]
    groups = tokens // GROUP
    width_out = out_ref.shape[1]
    load = pltpu.make_async_copy(w_hbm, w_s, sem)

    @pl.when(pair == 0)
    def _():
        load.start()

    first_half = iota((GROUP, 128), 1) < 64
    top_half = iota((128, 128), 0) < 64
    same = (iota((128, 128), 0) < 64) == (iota((128, 128), 1) < 64)
    block = jnp.where(same, 1.0 / 64.0, 0.0).astype(BF16)
    e0, e1 = pair_columns(ecol_ref[...], pair)
    base = ent_ref[...].astype(F32)
    before = jnp.ones((128, 128), F32)
    for c in range(groups):
        span = slice(c * GROUP, (c + 1) * GROUP)
        entry = (before * base + prefix_ref[c - 1]).astype(BF16) if c else ent_ref[...]
        end = (c + 1) * GROUP
        before = before * jnp.where(top_half, e0[end - 1 : end, :], e1[end - 1 : end, :])
        carried = nt(c_ref[span, :], entry)
        carried = carried * jnp.where(first_half, e0[span, :], e1[span, :])
        gate = gate_ref[span, :].astype(F32)
        g = (inside_ref[span, :] + carried) * (gate / (1.0 + jnp.exp(-gate)))
        square = g * g
        high = square.astype(BF16)
        low = (square - high.astype(F32)).astype(BF16)
        mean = nn(high, block) + nn(low, block)
        normed = g * lax.rsqrt(mean + EPS) * gain_ref[...]
        normed_s[span, pl.ds(pl.multiple_of(pair * 128, 128), 128)] = normed.astype(BF16)

    @pl.when(pair == pl.num_programs(0) - 1)
    def _():
        load.wait()

        @pl.loop(0, width_out // 256)
        def _(n):
            cols = pl.ds(pl.multiple_of(n * 256, 256), 256)
            out_ref[:, cols] = nn(normed_s[...], w_s[:, cols]).astype(BF16)


def token_part(inside, gate, ent, prefix, ecol, c, gain, w):
    tokens, width = inside.shape
    pairs = width // 128
    whole = lambda shape: pl.BlockSpec(shape, lambda p: (0,) * len(shape))
    lanes = lambda rows: pl.BlockSpec((rows, 128), lambda p: (0, p))
    return pl.pallas_call(
        token_kernel,
        grid=(pairs,),
        in_specs=[
            lanes(tokens),
            lanes(tokens),
            pl.BlockSpec((128, 128), lambda p: (p, 0)),
            pl.BlockSpec((prefix.shape[0], 128, 128), lambda p: (0, p, 0)),
            whole(ecol.shape),
            whole(c.shape),
            lanes(1),
            pl.BlockSpec(memory_space=pl.ANY),
        ],
        out_specs=whole((tokens, w.shape[1])),
        out_shape=jax.ShapeDtypeStruct((tokens, w.shape[1]), BF16),
        scratch_shapes=[
            VMEM((tokens, width), BF16),
            VMEM(w.shape, BF16),
            pltpu.SemaphoreType.DMA,
        ],
        compiler_params=pltpu.CompilerParams(vmem_limit_bytes=40 * 1024 * 1024),
        name="token_part",
    )(inside, gate, ent, prefix, ecol, c, gain, w)


def swap_kernel(bands, tile_ref, mine_ref, out_ref, got_s, sem):
    band, view = lax.axis_index("seq"), lax.axis_index("view")
    barrier = pltpu.get_barrier_semaphore()

    def to(j):
        return {"seq": j, "view": view}

    for d in range(1, bands):
        pl.semaphore_signal(
            barrier, inc=1, device_id=to(lax.rem(band + d, bands)), device_id_type=MESH
        )
    pl.semaphore_wait(barrier, bands - 1)

    def copy(source, target, d, j):
        return pltpu.make_async_remote_copy(
            src_ref=source, dst_ref=target, send_sem=sem.at[0, d], recv_sem=sem.at[1, d],
            device_id=to(j), device_id_type=MESH,
        )

    sends = []
    for d in sorted(range(1, bands), key=lambda d: -min(d, bands - d)):
        j = lax.rem(band + d, bands)
        sends.append(copy(mine_ref.at[j], got_s.at[band], d, j))
        sends[-1].start()
    got_s[band] = mine_ref[band]
    for d in range(1, bands):
        i = lax.rem(band - d + bands, bands)
        copy(mine_ref.at[i], got_s.at[i], d, i).wait_recv()
    for k in range(out_ref.shape[0]):
        per = out_ref.shape[1]
        tile = tile_ref[0, k]
        for u in range(per):
            out_ref[k, u] = got_s[tile * per + u]
    for sent in sends:
        sent.wait_send()


def swap_part(tiles, projected, bands):
    tokens, width = projected.shape
    piece = tokens // bands
    per = TILE // piece
    vmem = pl.BlockSpec(memory_space=pltpu.VMEM)
    return pl.pallas_call(
        functools.partial(swap_kernel, bands),
        in_specs=[pl.BlockSpec(memory_space=pltpu.SMEM), vmem],
        out_specs=vmem,
        out_shape=jax.ShapeDtypeStruct((tokens // TILE, per, piece, width), BF16),
        scratch_shapes=[
            VMEM((bands, piece, width), BF16),
            pltpu.SemaphoreType.DMA((2, bands)),
        ],
        compiler_params=pltpu.CompilerParams(collective_id=1, has_side_effects=True),
        name="swap_part",
    )(tiles, projected.reshape(bands, piece, width))


def shards(
    ssd_input, gate_input, b_matrix, c_matrix, log_decay,
    d_skip, norm_gain, out_weight, view_order, tile_order,
):
    views, bands = lax.axis_size("view"), lax.axis_size("seq")
    x, gate = ssd_input[0, 0], gate_input[0, 0]
    b, c, ld = b_matrix[0, 0], c_matrix[0, 0], log_decay[0, 0]
    tokens, width = x.shape
    skip = jnp.repeat(d_skip, width // d_skip.shape[0])[None, :]
    inside, state, prefix, ecol, total = local_part(x, b, c, ld, skip)
    ent = scan_part(view_order, state, total, views, bands).reshape(width, 128)
    projected = token_part(inside, gate, ent, prefix, ecol, c, norm_gain[None, :], out_weight)
    out = swap_part(tile_order, projected, bands)
    return out.reshape(1, 1, tokens, out_weight.shape[1])


def solution(mesh):
    whole = P("seq", "view", None, None)
    in_specs = (whole,) * 5 + (P(), P(), P(), P("seq", None), P("seq", None))
    return jax.shard_map(
        shards, mesh=mesh, in_specs=in_specs, out_specs=whole, check_vma=False
    )
```

time: 225 us -> 112 us (0.50)
  the two profiles are of different devices: /device:TPU:0 before, /device:TPU:13 now
where the time goes in v1:
time: 112 us; the launch traced here: 111 us
  Pallas kernels  99.8 us (89%)
  local copies, waits for them, and re-layouts  10.7 us (10%)
    pallas_call x1, Pallas kernels, swap_part(): pl.pallas_call(functools.partial(swap_kernel, bands), in_specs=[pl.BlockS...  40.6 us
    pallas_call x1, Pallas kernels, scan_part(): pl.pallas_call(functools.partial(scan_kernel, views, pack, groups, share)...  27 us
    pallas_call x1, Pallas kernels, local_part(): pl.pallas_call(local_kernel, grid=(pairs,), in_specs=[lanes(tokens), whol...  17.5 us
    pallas_call x1, Pallas kernels, token_part(): pl.pallas_call(token_kernel, grid=(pairs,), in_specs=[lanes(tokens), lane...  14.7 us
    unnamed x17, local copies, waits for them, and re-layouts  9.2 us

profile of v1, /device:TPU:13, one launch (start us, length us, event | category | flops | bytes accessed | tf_op | source)
XLA Modules:
  0.0 110.6 jit_solution(16428889066426535501)
XLA Ops:
  0.0 0.0 copy-start.7
  0.0 0.0 copy-start.5
  0.0 0.0 copy-start.2
  0.0 0.9 broadcast_in_dim.6
  0.9 0.7 broadcast_in_dim_reshape.3.skip_ref
  1.6 17.5 %local_part.1 = (f32[512,2048]{1,0:T(8,128)}, bf16[2048,128]{1,0:T(8,128)(2,1)}, f32[1,2048,128]{2,1,0:T(8,128)}, f32[512,128]{1,0:T(8,128)}, f32[32,128]{1,0:T(8,128)}) custom-call(bf16[512,2048]{1,0:T(8,128)(2,1)} %bitcast.17, bf16[512,128]{1,0:T(8,128)(2,1)} %bitcast.19, bf16[512,128]{1,0:T(8,128)(2,1)} %bitcast.13, f32[32,512]{1,0:T(8,128)} %bitcast.20, ...), custom_call_target="tpu_custom_call" | custom-call | tf_op jit(solution)/shard_map/local_part/pallas_call | solution.py:113
  19.0 27.0 %scan_part.1 = bf16[8,256,128]{2,1,0:T(8,128)(2,1)} custom-call(s32[1,4]{1,0:T(1,128)} %order_ref.1, bf16[8,256,128]{2,1,0:T(8,128)(2,1)} %bitcast.18, f32[32,128]{1,0:T(8,128)} %get-tuple-element.12.total_ref), custom_call_target="tpu_custom_call" | custom-call | tf_op jit(solution)/shard_map/scan_part/pallas_call | solution.py:299
  46.0 0.0 copy-done.7
  46.0 0.0 copy-done.5
  46.0 0.0 copy-done.2
  46.0 0.0 copy-start.1
  46.0 2.2 %copy-done.1 = f32[512,2048]{1,0:T(8,128)S(1)} copy-done((f32[512,2048]{1,0:T(8,128)S(1)}, f32[512,2048]{1,0:T(8,128)}, u32[]{:S(2)}) %copy-start.1) | copy-done | bytes 4194328
  48.2 0.0 copy-start.3
  48.2 1.0 copy-done.3
  49.3 0.0 copy-start.4
  49.3 1.2 %copy-done.4 = f32[1,2048,128]{2,1,0:T(8,128)S(1)} copy-done((f32[1,2048,128]{2,1,0:T(8,128)S(1)}, f32[1,2048,128]{2,1,0:T(8,128)}, u32[]{:S(2)}) %copy-start.4) | copy-done | bytes 1048600
  50.5 0.0 copy-start.6
  50.5 0.9 copy-done.6
  51.4 14.7 %token_part.1 = bf16[512,1536]{1,0:T(8,128)(2,1)S(1)} custom-call(f32[512,2048]{1,0:T(8,128)S(1)} %copy-done.1, bf16[512,2048]{1,0:T(8,128)(2,1)S(1)} %bitcast.11, bf16[2048,128]{1,0:T(8,128)(2,1)S(1)} %bitcast.12, f32[1,2048,128]{2,1,0:T(8,128)S(1)} %copy-done.4, f32[512,128]{1,0:T(8,128)S(1)} %copy-done.6, bf16[512,128]{1,0:T(8,128)(2,1)S(1)} %bitcast.14, ...), custom_call_target="tpu_custom_call" | custom-call | tf_op jit(solution)/shard_map/token_part/pallas_call | solution.py:374
  66.2 0.0 copy-start
  66.2 1.1 %copy-done = bf16[512,1536]{1,0:T(8,128)(2,1)} copy-done((bf16[512,1536]{1,0:T(8,128)(2,1)}, bf16[512,1536]{1,0:T(8,128)(2,1)S(1)}, u32[]{:S(2)}) %copy-start) | copy-done | bytes 1572888
  67.3 40.6 %swap_part.1 = bf16[4,2,64,1536]{3,2,1,0:T(8,128)(2,1)} custom-call(s32[1,4]{1,0:T(1,128)} %tile_ref.1, bf16[8,64,1536]{2,1,0:T(8,128)(2,1)} %bitcast.10), custom_call_target="tpu_custom_call" | custom-call | tf_op jit(solution)/shard_map/swap_part/pallas_call | solution.py:441
  107.9 2.7 %copy.12 = bf16[1,1,512,1536]{3,2,1,0:T(8,128)(2,1)} copy(bf16[1,1,512,1536]{3,2,1,0:T(8,128)(2,1)} %bitcast.16) | data formatting | bytes 3145728
Async XLA Ops:
  0.0 46.0 %copy-start.7 = (f32[2048]{0:T(1024)S(1)}, f32[2048]{0:T(1024)}, u32[]{:S(2)}) copy-start(f32[2048]{0:T(1024)} %param.16) | copy-start | bytes 24580
  0.0 46.0 %copy-start.5 = (bf16[1,1,512,128]{3,2,1,0:T(8,128)(2,1)S(1)}, bf16[1,1,512,128]{3,2,1,0:T(8,128)(2,1)}, u32[]{:S(2)}) copy-start(bf16[1,1,512,128]{3,2,1,0:T(8,128)(2,1)} %param.13) | copy-start | bytes 393220
  0.0 46.0 %copy-start.2 = (bf16[1,1,512,2048]{3,2,1,0:T(8,128)(2,1)S(1)}, bf16[1,1,512,2048]{3,2,1,0:T(8,128)(2,1)}, u32[]{:S(2)}) copy-start(bf16[1,1,512,2048]{3,2,1,0:T(8,128)(2,1)} %param.11) | copy-start | bytes 6291460
  46.0 2.2 %copy-start.1 = (f32[512,2048]{1,0:T(8,128)S(1)}, f32[512,2048]{1,0:T(8,128)}, u32[]{:S(2)}) copy-start(f32[512,2048]{1,0:T(8,128)} %get-tuple-element.10.inside_ref) | copy-start | bytes 12582916
  48.2 1.0 copy-start.3
  49.3 1.2 %copy-start.4 = (f32[1,2048,128]{2,1,0:T(8,128)S(1)}, f32[1,2048,128]{2,1,0:T(8,128)}, u32[]{:S(2)}) copy-start(f32[1,2048,128]{2,1,0:T(8,128)} %get-tuple-element.13.prefix_ref) | copy-start | bytes 3145732
  50.5 0.9 copy-start.6
  66.2 1.1 %copy-start = (bf16[512,1536]{1,0:T(8,128)(2,1)}, bf16[512,1536]{1,0:T(8,128)(2,1)S(1)}, u32[]{:S(2)}) copy-start(bf16[512,1536]{1,0:T(8,128)(2,1)S(1)} %token_part.1) | copy-start | bytes 4718596

commit v2 on v1

v2 whole, which is shorter than its diff:
```python
import functools

import jax
import jax.numpy as jnp
from jax import lax
from jax.experimental import pallas as pl
from jax.experimental.pallas import tpu as pltpu
from jax.sharding import PartitionSpec as P

GROUP = 256
TILE = 128
EPS = 1e-05
MESH = pl.DeviceIdType.MESH
F32 = jnp.float32
BF16 = jnp.bfloat16
VMEM = pltpu.VMEM
VMEM_LIMIT = 64 * 1000 * 1000


def nn(a, b):
    return lax.dot_general(a, b, (((1,), (0,)), ((), ())), preferred_element_type=F32)


def nt(a, b):
    return lax.dot_general(a, b, (((1,), (1,)), ((), ())), preferred_element_type=F32)


def tn(a, b):
    return lax.dot_general(a, b, (((0,), (0,)), ((), ())), preferred_element_type=F32)


def split3(a):
    hi = a.astype(BF16)
    rest = a - hi.astype(F32)
    mid = rest.astype(BF16)
    low = (rest - mid.astype(F32)).astype(BF16)
    return hi, mid, low


def iota(shape, dim):
    return lax.broadcasted_iota(jnp.int32, shape, dim)


def pair_columns(full, pair):
    lanes = full.shape[1]
    turned = pltpu.roll(full, lax.rem(lanes - 2 * pair, lanes), 1)
    return turned[:, 0:1], turned[:, 1:2]


def local_kernel(
    x_ref, b_ref, c_ref, ld_ref,
    state_ref, prefix_ref, col_ref, row_ref, score_ref, total_ref,
    scale_s,
):
    step = pl.program_id(0)
    heads, tokens = ld_ref.shape
    groups = tokens // GROUP
    pairs = x_ref.shape[1] // 128

    @pl.when(step == 0)
    def _():
        at_row, at_col = iota((GROUP, GROUP), 0), iota((GROUP, GROUP), 1)
        lower = jnp.where(at_col <= at_row, 1.0, 0.0).astype(BF16)
        upper = jnp.where(at_row <= at_col, 1.0, 0.0).astype(BF16)
        total = jnp.zeros((heads, 1), F32)
        for c in range(groups):
            span = slice(c * GROUP, (c + 1) * GROUP)
            own = ld_ref[:, span]
            padded = jnp.concatenate([own, jnp.zeros((128 - heads, GROUP), F32)], axis=0)
            rows = sum(nn(part, upper) for part in split3(own))
            row_ref[:, span] = rows
            cols = sum(nt(lower, part) for part in split3(padded))
            col_ref[span, :] = cols
            scale_s[span, :] = jnp.exp(jnp.minimum(cols[GROUP - 1 : GROUP, :] - cols, 0.0))
            total = total + rows[:, GROUP - 1 : GROUP]
            scores = nt(c_ref[span, :], b_ref[span, :])
            score_ref[c] = jnp.where(at_col <= at_row, scores, 0.0)
        total_ref[...] = jnp.broadcast_to(total, total_ref.shape)

    top_half = iota((128, 128), 0) < 64
    for j in range(pairs):
        pair = step * pairs + j
        at = slice(j * 128, (j + 1) * 128)
        f0, f1 = pair_columns(scale_s[...], pair)
        running = jnp.zeros((128, 128), F32)
        for c in range(groups):
            span = slice(c * GROUP, (c + 1) * GROUP)
            bf = b_ref[span, :].astype(F32)
            scaled = jnp.concatenate(
                [(f0[span, :] * bf).astype(BF16), (f1[span, :] * bf).astype(BF16)], axis=1
            )
            both = tn(x_ref[span, at], scaled)
            state = jnp.where(top_half, both[:, 0:128], both[:, 128:256])
            if c:
                prefix_ref[c - 1, at, :] = running
            e0 = row_ref[pl.ds(2 * pair, 1), span][:, GROUP - 1 : GROUP]
            e1 = row_ref[pl.ds(2 * pair + 1, 1), span][:, GROUP - 1 : GROUP]
            running = jnp.exp(jnp.where(top_half, e0, e1)) * running + state
        state_ref[at, :] = running.astype(BF16)


def local_part(x, b, c, ld):
    tokens, width = x.shape
    heads = ld.shape[0]
    groups = tokens // GROUP
    block = 512
    whole = lambda shape: pl.BlockSpec(shape, lambda p: (0,) * len(shape))
    shapes = [
        ((width, 128), BF16, pl.BlockSpec((block, 128), lambda p: (p, 0))),
        ((groups - 1, width, 128), F32, pl.BlockSpec((groups - 1, block, 128), lambda p: (0, p, 0))),
        ((tokens, 128), F32, whole((tokens, 128))),
        ((heads, tokens), F32, whole((heads, tokens))),
        ((groups, GROUP, GROUP), F32, whole((groups, GROUP, GROUP))),
        ((heads, 128), F32, whole((heads, 128))),
    ]
    return pl.pallas_call(
        local_kernel,
        grid=(width // block,),
        in_specs=[
            pl.BlockSpec((tokens, block), lambda p: (0, p)),
            whole(b.shape), whole(c.shape), whole(ld.shape),
        ],
        out_specs=[spec for _, _, spec in shapes],
        out_shape=[jax.ShapeDtypeStruct(shape, dtype) for shape, dtype, _ in shapes],
        scratch_shapes=[VMEM((tokens, 128), F32)],
        compiler_params=pltpu.CompilerParams(vmem_limit_bytes=VMEM_LIMIT),
        name="local_part",
    )(x, b, c, ld)


def scan_kernel(
    views, pack, groups, share,
    order_ref, state_ref, total_ref, skip_ref, col_ref, row_ref, score_ref, x_hbm,
    out_ref, inside_hbm,
    x_s, inside_s, sem_x, sem_i, note_s, got_s, gotnote_s, agg_s, aggnote_s, aggs_s, aggnotes_s, within_s, before_s, send_s,
    sem_a, sem_an, sem_b, sem_bn, sem_c,
):
    band, view = lax.axis_index("seq"), lax.axis_index("view")
    count = views * pack
    group, member = band // pack, lax.rem(band, pack)
    me = member * views + view
    rows = share * 64

    pairs = x_s.shape[1] // 128
    cuts = [0, pairs * 3 // 8, pairs * 11 // 16, pairs]
    load = pltpu.make_async_copy(x_hbm, x_s, sem_x)
    load.start()
    first_half = iota((GROUP, 128), 1) < 64

    def inside_span(part):
        @pl.loop(cuts[part], cuts[part + 1])
        def _(pair):
            cols = pair_columns(col_ref[...], pair)
            lanes = pl.ds(pl.multiple_of(pair * 128, 128), 128)
            for c in range(x_s.shape[0] // GROUP):
                span = slice(c * GROUP, (c + 1) * GROUP)
                x = x_s[span, lanes]
                outs = []
                for j, col in enumerate(cols):
                    line = row_ref[pl.ds(2 * pair + j, 1), span]
                    gap = jnp.minimum(col[span, :] - line, 0.0)
                    outs.append(nn((jnp.exp(gap) * score_ref[c]).astype(BF16), x))
                inside_s[span, lanes] = (
                    jnp.where(first_half, outs[0], outs[1])
                    + jnp.where(first_half, skip_ref[2 * pair], skip_ref[2 * pair + 1]) * x.astype(F32)
                )

        lanes = pl.ds(cuts[part] * 128, (cuts[part + 1] - cuts[part]) * 128)
        copy = pltpu.make_async_copy(
            inside_s.at[:, lanes], inside_hbm.at[:, lanes], sem_i.at[part]
        )
        copy.start()
        return copy

    def peer(q):
        return {"seq": group * pack + q // views, "view": lax.rem(q, views)}

    def across(g):
        return {"seq": g * pack + member, "view": view}

    barrier = pltpu.get_barrier_semaphore()
    for d in range(1, count):
        pl.semaphore_signal(
            barrier, inc=1, device_id=peer(lax.rem(me + d, count)), device_id_type=MESH
        )
    for d in range(1, groups):
        pl.semaphore_signal(
            barrier, inc=1, device_id=across(lax.rem(group + d, groups)), device_id_type=MESH
        )
    rank = jnp.int32(0)
    for r in range(views):
        rank = rank + jnp.where(order_ref[0, r] == view, r, 0)
    key = (rank + member * views).astype(F32)
    for q in range(count):
        note_s[q, 0:share, :] = total_ref[q * share : (q + 1) * share, :]
        note_s[q, share : share + 1, :] = jnp.full((1, 128), key, F32)
    pl.semaphore_wait(barrier, count - 1 + groups - 1)

    def exchange(source, target, sem, d, q):
        return pltpu.make_async_remote_copy(
            src_ref=source, dst_ref=target, send_sem=sem.at[0, d], recv_sem=sem.at[1, d],
            device_id=peer(q), device_id_type=MESH,
        )

    sends = []
    for d in range(1, count):
        q = lax.rem(me + d, count)
        sends.append(exchange(note_s.at[q], gotnote_s.at[me], sem_an, d, q))
        sends[-1].start()
        sends.append(exchange(state_ref.at[q], got_s.at[me], sem_a, d, q))
        sends[-1].start()
    got_s[me] = state_ref[me]
    gotnote_s[me] = note_s[me]
    load.wait()
    saved = [inside_span(0)]
    for d in range(1, count):
        src = lax.rem(me - d + count, count)
        exchange(note_s.at[src], gotnote_s.at[src], sem_an, d, src).wait_recv()
        exchange(state_ref.at[src], got_s.at[src], sem_a, d, src).wait_recv()

    logs = [gotnote_s[b] for b in range(count)]
    keys = [jnp.broadcast_to(log[share : share + 1, :], log.shape) for log in logs]
    zero = jnp.zeros_like(logs[0])
    before, upto, whole = [], [], zero
    for b in range(count):
        acc = zero
        for o in range(count):
            if o != b:
                acc = acc + jnp.where(keys[o] < keys[b], logs[o], 0.0)
        before.append(acc)
        upto.append(acc + logs[b])
        before_s[b] = jnp.exp(acc)
        whole = whole + logs[b]
    aggnote_s[...] = whole
    last = [jnp.exp(jnp.minimum(whole - upto[b], 0.0)) for b in range(count)]
    for i in range(share):
        span = slice(i * 64, (i + 1) * 64)
        acc = jnp.zeros((64, 128), F32)
        for b in range(count):
            acc = acc + last[b][i : i + 1, :] * got_s[b, span, :].astype(F32)
        agg_s[span, :] = acc.astype(BF16)

    def ahead(source, target, sem, k, g):
        return pltpu.make_async_remote_copy(
            src_ref=source, dst_ref=target, send_sem=sem.at[0, k], recv_sem=sem.at[1, k],
            device_id=across(g), device_id_type=MESH,
        )

    def ahead_pair(k, g):
        return (
            ahead(aggnote_s, aggnotes_s.at[k], sem_bn, k, g),
            ahead(agg_s, aggs_s.at[k], sem_b, k, g),
        )

    for k in range(groups - 1, 0, -1):
        @pl.when(group + k < groups)
        def _(k=k):
            for copy in ahead_pair(k, group + k):
                copy.start()

    for b in range(count):
        coefs = [
            jnp.where(
                keys[o] < keys[b], jnp.exp(jnp.minimum(before[b] - upto[o], 0.0)), 0.0
            )
            for o in range(count)
            if o != b
        ]
        others = [o for o in range(count) if o != b]
        for i in range(share):
            span = slice(i * 64, (i + 1) * 64)
            acc = jnp.zeros((64, 128), F32)
            for o, coef in zip(others, coefs):
                acc = acc + coef[i : i + 1, :] * got_s[o, span, :].astype(F32)
            within_s[b, span, :] = acc

    saved.append(inside_span(1))
    carry = within_s.at[count]
    carry[...] = jnp.zeros((rows, 128), F32)
    for k in range(groups - 1, 0, -1):
        @pl.when(group - k >= 0)
        def _(k=k):
            for copy in ahead_pair(k, group - k):
                copy.wait_recv()
            decay = jnp.exp(aggnotes_s[k])
            for i in range(share):
                span = slice(i * 64, (i + 1) * 64)
                carry[span, :] = decay[i : i + 1, :] * carry[span, :] + aggs_s[k, span, :].astype(F32)

    def entering(q):
        factor = before_s[q]
        parts = []
        for i in range(share):
            span = slice(i * 64, (i + 1) * 64)
            parts.append(factor[i : i + 1, :] * carry[span, :] + within_s[q, span, :])
        return jnp.concatenate(parts, axis=0).astype(BF16)

    for d in range(1, count):
        q = lax.rem(me + d, count)
        send_s[d] = entering(q)
        sends.append(exchange(send_s.at[d], out_ref.at[me], sem_c, d, q))
        sends[-1].start()
    out_ref[me] = entering(me)
    saved.append(inside_span(2))
    for d in range(1, count):
        src = lax.rem(me - d + count, count)
        exchange(send_s.at[d], out_ref.at[src], sem_c, d, src).wait_recv()
    for copy in sends:
        copy.wait_send()
    for k in range(1, groups):
        @pl.when(group + k < groups)
        def _(k=k):
            for copy in ahead_pair(k, group + k):
                copy.wait_send()
    for copy in saved:
        copy.wait()


def scan_part(order, state, total, col, row, score, skip, x, views, bands):
    heads = total.shape[0]
    pack = 2 if bands % 2 == 0 and heads % (2 * views) == 0 else 1
    count = views * pack
    share = heads // count
    groups = bands // pack
    rows = share * 64
    vmem = pl.BlockSpec(memory_space=pltpu.VMEM)
    hbm = pl.BlockSpec(memory_space=pl.ANY)
    smem = pl.BlockSpec(memory_space=pltpu.SMEM)
    sems = lambda n: pltpu.SemaphoreType.DMA((2, n))
    return pl.pallas_call(
        functools.partial(scan_kernel, views, pack, groups, share),
        in_specs=[smem] + [vmem] * 2 + [smem] + [vmem] * 3 + [hbm],
        out_specs=[vmem, hbm],
        out_shape=[
            jax.ShapeDtypeStruct((count, rows, 128), BF16),
            jax.ShapeDtypeStruct(x.shape, F32),
        ],
        scratch_shapes=[
            VMEM(x.shape, BF16),
            VMEM(x.shape, F32),
            pltpu.SemaphoreType.DMA,
            pltpu.SemaphoreType.DMA((3,)),
            VMEM((count, 8, 128), F32),
            VMEM((count, rows, 128), BF16),
            VMEM((count, 8, 128), F32),
            VMEM((rows, 128), BF16),
            VMEM((8, 128), F32),
            VMEM((groups, rows, 128), BF16),
            VMEM((groups, 8, 128), F32),
            VMEM((count + 1, rows, 128), F32),
            VMEM((count, 8, 128), F32),
            VMEM((count, rows, 128), BF16),
            sems(count), sems(count), sems(groups), sems(groups), sems(count),
        ],
        compiler_params=pltpu.CompilerParams(
            collective_id=0, has_side_effects=True, vmem_limit_bytes=VMEM_LIMIT
        ),
        name="scan_part",
    )(order, state.reshape(count, rows, 128), total, skip, col, row, score, x)


def token_kernel(
    bands, tile_ref, ent_ref, prefix_ref, col_ref, c_ref, gain_ref, inside_hbm, gate_hbm, w_hbm,
    out_ref,
    inside_s, gate_s, w_s, ecol_s, entry_s, normed_s, mine_s, got_s, load_sem, w_sem, sem,
):
    band, view = lax.axis_index("seq"), lax.axis_index("view")
    tokens, width = inside_s.shape
    width_out = w_s.shape[1]
    groups = tokens // GROUP
    pairs = width // 128
    piece = mine_s.shape[1]
    chunk = max(piece, TILE)
    chunks = tokens // chunk
    per_chunk = chunk // piece
    shift = (1 - band // (bands // 2)) * (chunks // 2)

    def chunk_of(i):
        return lax.rem(shift + i, chunks)

    def rows_of(i):
        return pl.ds(pl.multiple_of(chunk_of(i) * chunk, chunk), chunk)

    def loads(i):
        rows = rows_of(i)
        return (
            pltpu.make_async_copy(inside_hbm.at[rows], inside_s.at[rows], load_sem.at[0, i]),
            pltpu.make_async_copy(gate_hbm.at[rows], gate_s.at[rows], load_sem.at[1, i]),
        )

    load_w = pltpu.make_async_copy(w_hbm, w_s, w_sem)
    for copy in loads(0):
        copy.start()
    load_w.start()
    for i in range(1, chunks):
        for copy in loads(i):
            copy.start()

    barrier = pltpu.get_barrier_semaphore()

    def to(j):
        return {"seq": j, "view": view}

    for d in range(1, bands):
        pl.semaphore_signal(
            barrier, inc=1, device_id=to(lax.rem(band + d, bands)), device_id_type=MESH
        )

    ecol_s[...] = jnp.exp(col_ref[...])
    top_half = iota((128, 128), 0) < 64

    @pl.loop(0, pairs)
    def _(pair):
        rows = pl.ds(pl.multiple_of(pair * 128, 128), 128)
        mine = ent_ref[rows, :]
        entry_s[0, rows, :] = mine
        before = jnp.ones((128, 128), F32)
        for c in range(1, groups):
            e0, e1 = pair_columns(ecol_s[c * GROUP - 8 : c * GROUP, :], pair)
            before = before * jnp.where(top_half, e0[7:8, :], e1[7:8, :])
            entry = before * mine.astype(F32) + prefix_ref[c - 1, rows, :]
            entry_s[c, rows, :] = entry.astype(BF16)

    pl.semaphore_wait(barrier, bands - 1)

    def send(j):
        return pltpu.make_async_remote_copy(
            src_ref=mine_s.at[j], dst_ref=got_s.at[band],
            send_sem=sem.at[0, j], recv_sem=sem.at[1, band],
            device_id=to(j), device_id_type=MESH,
        )

    def arrival(i):
        return pltpu.make_async_remote_copy(
            src_ref=mine_s.at[i], dst_ref=got_s.at[i],
            send_sem=sem.at[0, i], recv_sem=sem.at[1, i],
            device_id=to(i), device_id_type=MESH,
        )

    first_half = iota((chunk, 128), 1) < 64
    same = (iota((128, 128), 0) < 64) == (iota((128, 128), 1) < 64)
    block = jnp.where(same, 1.0 / 64.0, 0.0).astype(BF16)
    for i in range(chunks):
        rows = rows_of(i)
        group = chunk_of(i) * chunk // GROUP
        for copy in loads(i):
            copy.wait()

        def one(pair):
            lanes = pl.ds(pl.multiple_of(pair * 128, 128), 128)
            e0, e1 = pair_columns(ecol_s[rows, :], pair)
            carried = nt(c_ref[rows, :], entry_s[group, lanes, :])
            carried = carried * jnp.where(first_half, e0, e1)
            gate = gate_s[rows, lanes].astype(F32)
            g = (inside_s[rows, lanes] + carried) * (gate / (1.0 + jnp.exp(-gate)))
            square = g * g
            high = square.astype(BF16)
            low = (square - high.astype(F32)).astype(BF16)
            mean = nn(high, block) + nn(low, block)
            normed = g * lax.rsqrt(mean + EPS) * gain_ref[:, lanes]
            normed_s[:, lanes] = normed.astype(BF16)

        @pl.loop(0, pairs // 4)
        def _(quad):
            for k in range(4):
                one(quad * 4 + k)

        if i == 0:
            load_w.wait()
        base = chunk_of(i) * per_chunk

        @pl.loop(0, width_out // 256)
        def _(n):
            cols = pl.ds(pl.multiple_of(n * 256, 256), 256)
            made = nn(normed_s[...], w_s[:, cols])
            for u in range(per_chunk):
                mine_s[base + u, :, cols] = made[u * piece : (u + 1) * piece, :].astype(BF16)

        for u in range(per_chunk):
            j = base + u

            @pl.when(j != band)
            def _(j=j):
                send(j).start()

    got_s[band] = mine_s[band]
    for d in range(1, bands):
        arrival(lax.rem(band - d + bands, bands)).wait_recv()
    for k in range(out_ref.shape[0]):
        per = out_ref.shape[1]
        tile = tile_ref[0, k]
        for u in range(per):
            out_ref[k, u] = got_s[tile * per + u]
    for d in range(1, bands):
        send(lax.rem(band + d, bands)).wait_send()


def token_part(tiles, ent, prefix, col, c, gain, inside, gate, w, bands):
    tokens, width = inside.shape
    width_out = w.shape[1]
    piece = tokens // bands
    chunk = max(piece, TILE)
    vmem = pl.BlockSpec(memory_space=pltpu.VMEM)
    hbm = pl.BlockSpec(memory_space=pl.ANY)
    return pl.pallas_call(
        functools.partial(token_kernel, bands),
        in_specs=[pl.BlockSpec(memory_space=pltpu.SMEM)] + [vmem] * 5 + [hbm] * 3,
        out_specs=vmem,
        out_shape=jax.ShapeDtypeStruct((tokens // TILE, TILE // piece, piece, width_out), BF16),
        scratch_shapes=[
            VMEM((tokens, width), F32),
            VMEM((tokens, width), BF16),
            VMEM(w.shape, BF16),
            VMEM((tokens, 128), F32),
            VMEM((tokens // GROUP, width, 128), BF16),
            VMEM((chunk, width), BF16),
            VMEM((bands, piece, width_out), BF16),
            VMEM((bands, piece, width_out), BF16),
            pltpu.SemaphoreType.DMA((2, tokens // chunk)),
            pltpu.SemaphoreType.DMA,
            pltpu.SemaphoreType.DMA((2, bands)),
        ],
        compiler_params=pltpu.CompilerParams(
            collective_id=1, has_side_effects=True, vmem_limit_bytes=VMEM_LIMIT
        ),
        name="token_part",
    )(tiles, ent, prefix, col, c, gain, inside, gate, w)


def shards(
    ssd_input, gate_input, b_matrix, c_matrix, log_decay,
    d_skip, norm_gain, out_weight, view_order, tile_order,
):
    views, bands = lax.axis_size("view"), lax.axis_size("seq")
    x, gate = ssd_input[0, 0], gate_input[0, 0]
    b, c, ld = b_matrix[0, 0], c_matrix[0, 0], log_decay[0, 0]
    tokens, width = x.shape
    state, prefix, col, row, score, total = local_part(x, b, c, ld)
    ent, inside = scan_part(view_order, state, total, col, row, score, d_skip, x, views, bands)
    out = token_part(
        tile_order, ent.reshape(width, 128), prefix, col, c, norm_gain[None, :],
        inside, gate, out_weight, bands,
    )
    return out.reshape(1, 1, tokens, out_weight.shape[1])


def solution(mesh):
    whole = P("seq", "view", None, None)
    in_specs = (whole,) * 5 + (P(), P(), P(), P("seq", None), P("seq", None))
    return jax.shard_map(
        shards, mesh=mesh, in_specs=in_specs, out_specs=whole, check_vma=False
    )
```

time: 112 us -> 87.9 us (0.78)
  the two profiles are of different devices: /device:TPU:13 before, /device:TPU:29 now
where the time goes in v2:
time: 87.9 us; the launch traced here: 87.7 us
  Pallas kernels  85 us (97%)
  local copies, waits for them, and re-layouts  2.65 us (3%)
    pallas_call x1, Pallas kernels, token_part(): pl.pallas_call(functools.partial(token_kernel, bands), in_specs=[pl.Block...  50 us
    pallas_call x1, Pallas kernels, scan_part(): pl.pallas_call(functools.partial(scan_kernel, views, pack, groups, share)...  26.4 us
    pallas_call x1, Pallas kernels, local_part(): pl.pallas_call(local_kernel, grid=(width // block,), in_specs=[pl.BlockSp...  8.65 us
    unnamed x1, local copies, waits for them, and re-layouts  2.65 us

profile of v2, /device:TPU:29, one launch (start us, length us, event | category | flops | bytes accessed | tf_op | source)
XLA Modules:
  0.0 87.7 jit_solution(14108164140123441714)
XLA Ops:
  0.0 8.6 %local_part.1 = (bf16[2048,128]{1,0:T(8,128)(2,1)}, f32[1,2048,128]{2,1,0:T(8,128)}, f32[512,128]{1,0:T(8,128)}, f32[32,512]{1,0:T(8,128)}, f32[2,256,256]{2,1,0:T(8,128)}, /*index=5*/f32[32,128]{1,0:T(8,128)}) custom-call(bf16[512,2048]{1,0:T(8,128)(2,1)} %bitcast.9, bf16[512,128]{1,0:T(8,128)(2,1)} %bitcast.17, bf16[512,128]{1,0:T(8,128)(2,1)} %bitcast.13, ...), custom_call_target="tpu_custom_call" | custom-call | tf_op jit(solution)/shard_map/local_part/pallas_call | solution.py:116
  8.7 26.4 %scan_part.1 = (bf16[8,256,128]{2,1,0:T(8,128)(2,1)}, f32[512,2048]{1,0:T(8,128)}) custom-call(s32[1,4]{1,0:T(1,128)} %order_ref.1, bf16[8,256,128]{2,1,0:T(8,128)(2,1)} %bitcast.15, f32[32,128]{1,0:T(8,128)} %get-tuple-element.14.total_ref, f32[32]{0:T(128)} %skip_ref.1, f32[512,128]{1,0:T(8,128)} %get-tuple-element.15.col_ref, ...), custom_call_target="tpu_custom_call" | custom-call | tf_op jit(solution)/shard_map/scan_part/pallas_call | solution.py:330
  35.1 50.0 %token_part.1 = bf16[4,2,64,1536]{3,2,1,0:T(8,128)(2,1)} custom-call(s32[1,4]{1,0:T(1,128)} %tile_ref.1, bf16[2048,128]{1,0:T(8,128)(2,1)} %bitcast.16, f32[1,2048,128]{2,1,0:T(8,128)} %get-tuple-element.19.prefix_ref, f32[512,128]{1,0:T(8,128)} %get-tuple-element.15.col_ref, bf16[512,128]{1,0:T(8,128)(2,1)} %bitcast.14, f32[1,2048]{1,0:T(1,128)} %bitcast.19, ...), custom_call_target="tpu_custom_call" | custom-call | tf_op jit(solution)/shard_map/token_part/pallas_call | solution.py:505
  85.1 2.7 %copy.12 = bf16[1,1,512,1536]{3,2,1,0:T(8,128)(2,1)} copy(bf16[1,1,512,1536]{3,2,1,0:T(8,128)(2,1)} %bitcast.11) | data formatting | bytes 3145728

commit v3 on v2

v3 whole, which is shorter than its diff:
```python
import functools

import jax
import jax.numpy as jnp
from jax import lax
from jax.experimental import pallas as pl
from jax.experimental.pallas import tpu as pltpu
from jax.sharding import PartitionSpec as P

GROUP = 256
TILE = 128
EPS = 1e-05
MESH = pl.DeviceIdType.MESH
F32 = jnp.float32
BF16 = jnp.bfloat16
VMEM = pltpu.VMEM
VMEM_LIMIT = 64 * 1000 * 1000


def nn(a, b):
    return lax.dot_general(a, b, (((1,), (0,)), ((), ())), preferred_element_type=F32)


def nt(a, b):
    return lax.dot_general(a, b, (((1,), (1,)), ((), ())), preferred_element_type=F32)


def tn(a, b):
    return lax.dot_general(a, b, (((0,), (0,)), ((), ())), preferred_element_type=F32)


def split3(a):
    hi = a.astype(BF16)
    rest = a - hi.astype(F32)
    mid = rest.astype(BF16)
    low = (rest - mid.astype(F32)).astype(BF16)
    return hi, mid, low


def iota(shape, dim):
    return lax.broadcasted_iota(jnp.int32, shape, dim)


def pair_columns(full, pair):
    lanes = full.shape[1]
    turned = pltpu.roll(full, lax.rem(lanes - 2 * pair, lanes), 1)
    return turned[:, 0:1], turned[:, 1:2]


def mixer_kernel(
    views, pack, groups, share, bands,
    order_ref, skip_ref, b_ref, c_ref, ld_ref, gain_ref, x_hbm, gate_hbm, w_hbm,
    out_hbm,
    x_s, inside_s, gate_s, w_s, sem_x, sem_g, sem_w, sem_o,
    col_ref, row_ref, score_ref, scale_s, total_s, state_ref, prefix_ref, ent_s,
    note_s, got_s, gotnote_s, agg_s, aggnote_s, aggs_s, aggnotes_s, within_s, before_s, send_s,
    sem_a, sem_an, sem_b, sem_bn, sem_c,
    ecol_s, entry_s, normed_s, mine_s, sem,
):
    band, view = lax.axis_index("seq"), lax.axis_index("view")
    count = views * pack
    group, member = band // pack, lax.rem(band, pack)
    me = member * views + view
    rows = share * 64
    heads, tokens = ld_ref.shape
    spans = tokens // GROUP
    pairs = x_s.shape[1] // 128
    first_half = iota((GROUP, 128), 1) < 64
    top_half = iota((128, 128), 0) < 64

    load = pltpu.make_async_copy(x_hbm, x_s, sem_x)
    load_gate = pltpu.make_async_copy(gate_hbm, gate_s, sem_g)
    load_w = pltpu.make_async_copy(w_hbm, w_s, sem_w)
    load.start()
    load_gate.start()
    load_w.start()

    barrier = pltpu.get_barrier_semaphore()
    for d in range(1, bands):
        pl.semaphore_signal(
            barrier, inc=1,
            device_id={"seq": lax.rem(band + d, bands), "view": view}, device_id_type=MESH,
        )
    for d in range(1, views):
        for m in range(pack):
            pl.semaphore_signal(
                barrier, inc=1,
                device_id={"seq": group * pack + m, "view": lax.rem(view + d, views)},
                device_id_type=MESH,
            )

    at_row, at_col = iota((GROUP, GROUP), 0), iota((GROUP, GROUP), 1)
    lower = jnp.where(at_col <= at_row, 1.0, 0.0).astype(BF16)
    upper = jnp.where(at_row <= at_col, 1.0, 0.0).astype(BF16)
    total = jnp.zeros((heads, 1), F32)
    for c in range(spans):
        span = slice(c * GROUP, (c + 1) * GROUP)
        own = ld_ref[:, span]
        padded = jnp.concatenate([own, jnp.zeros((128 - heads, GROUP), F32)], axis=0)
        lines = sum(nn(part, upper) for part in split3(own))
        row_ref[:, span] = lines
        cols = sum(nt(lower, part) for part in split3(padded))
        col_ref[span, :] = cols
        ecol_s[span, :] = jnp.exp(cols)
        scale_s[span, :] = jnp.exp(jnp.minimum(cols[GROUP - 1 : GROUP, :] - cols, 0.0))
        total = total + lines[:, GROUP - 1 : GROUP]
        scores = nt(c_ref[span, :], b_ref[span, :])
        score_ref[c] = jnp.where(at_col <= at_row, scores, 0.0)
    total_s[...] = jnp.broadcast_to(total, total_s.shape)

    rank = jnp.int32(0)
    for r in range(views):
        rank = rank + jnp.where(order_ref[0, r] == view, r, 0)
    key = (rank + member * views).astype(F32)
    for q in range(count):
        note_s[q, 0:share, :] = total_s[q * share : (q + 1) * share, :]
        note_s[q, share : share + 1, :] = jnp.full((1, 128), key, F32)

    def states_of(q):
        for j in range(share // 2):
            pair = q * (share // 2) + j
            at = slice(j * 128, (j + 1) * 128)
            lanes = pl.ds(pl.multiple_of(pair * 128, 128), 128)
            f0, f1 = pair_columns(scale_s[...], pair)
            running = jnp.zeros((128, 128), F32)
            for c in range(spans):
                span = slice(c * GROUP, (c + 1) * GROUP)
                bf = b_ref[span, :].astype(F32)
                scaled = jnp.concatenate(
                    [(f0[span, :] * bf).astype(BF16), (f1[span, :] * bf).astype(BF16)], axis=1
                )
                both = tn(x_s[span, lanes], scaled)
                state = jnp.where(top_half, both[:, 0:128], both[:, 128:256])
                if c:
                    prefix_ref[c - 1, lanes, :] = running
                e0 = row_ref[pl.ds(2 * pair, 1), span][:, GROUP - 1 : GROUP]
                e1 = row_ref[pl.ds(2 * pair + 1, 1), span][:, GROUP - 1 : GROUP]
                running = jnp.exp(jnp.where(top_half, e0, e1)) * running + state
            state_ref[q, at, :] = running.astype(BF16)

    cuts = [0, pairs * 3 // 8, pairs * 11 // 16, pairs]
    def inside_span(part):
        @pl.loop(cuts[part], cuts[part + 1])
        def _(pair):
            cols = pair_columns(col_ref[...], pair)
            lanes = pl.ds(pl.multiple_of(pair * 128, 128), 128)
            for c in range(x_s.shape[0] // GROUP):
                span = slice(c * GROUP, (c + 1) * GROUP)
                x = x_s[span, lanes]
                outs = []
                for j, col in enumerate(cols):
                    line = row_ref[pl.ds(2 * pair + j, 1), span]
                    gap = jnp.minimum(col[span, :] - line, 0.0)
                    outs.append(nn((jnp.exp(gap) * score_ref[c]).astype(BF16), x))
                inside_s[span, lanes] = (
                    jnp.where(first_half, outs[0], outs[1])
                    + jnp.where(first_half, skip_ref[2 * pair], skip_ref[2 * pair + 1]) * x.astype(F32)
                )

    def peer(q):
        return {"seq": group * pack + q // views, "view": lax.rem(q, views)}

    def across(g):
        return {"seq": g * pack + member, "view": view}

    def exchange(source, target, sem, d, q):
        return pltpu.make_async_remote_copy(
            src_ref=source, dst_ref=target, send_sem=sem.at[0, d], recv_sem=sem.at[1, d],
            device_id=peer(q), device_id_type=MESH,
        )

    sends = []
    load.wait()
    pl.semaphore_wait(barrier, bands - 1 + (views - 1) * pack)
    for d in range(1, count):
        q = lax.rem(me + d, count)
        sends.append(exchange(note_s.at[q], gotnote_s.at[me], sem_an, d, q))
        sends[-1].start()
        states_of(q)
        sends.append(exchange(state_ref.at[q], got_s.at[me], sem_a, d, q))
        sends[-1].start()
    states_of(me)
    got_s[me] = state_ref[me]
    gotnote_s[me] = note_s[me]
    inside_span(0)
    for d in range(1, count):
        src = lax.rem(me - d + count, count)
        exchange(note_s.at[src], gotnote_s.at[src], sem_an, d, src).wait_recv()
        exchange(state_ref.at[src], got_s.at[src], sem_a, d, src).wait_recv()

    logs = [gotnote_s[b] for b in range(count)]
    keys = [jnp.broadcast_to(log[share : share + 1, :], log.shape) for log in logs]
    zero = jnp.zeros_like(logs[0])
    before, upto, whole = [], [], zero
    for b in range(count):
        acc = zero
        for o in range(count):
            if o != b:
                acc = acc + jnp.where(keys[o] < keys[b], logs[o], 0.0)
        before.append(acc)
        upto.append(acc + logs[b])
        before_s[b] = jnp.exp(acc)
        whole = whole + logs[b]
    aggnote_s[...] = whole
    last = [jnp.exp(jnp.minimum(whole - upto[b], 0.0)) for b in range(count)]
    for i in range(share):
        span = slice(i * 64, (i + 1) * 64)
        acc = jnp.zeros((64, 128), F32)
        for b in range(count):
            acc = acc + last[b][i : i + 1, :] * got_s[b, span, :].astype(F32)
        agg_s[span, :] = acc.astype(BF16)

    def ahead(source, target, sem, k, g):
        return pltpu.make_async_remote_copy(
            src_ref=source, dst_ref=target, send_sem=sem.at[0, k], recv_sem=sem.at[1, k],
            device_id=across(g), device_id_type=MESH,
        )

    def ahead_pair(k, g):
        return (
            ahead(aggnote_s, aggnotes_s.at[k], sem_bn, k, g),
            ahead(agg_s, aggs_s.at[k], sem_b, k, g),
        )

    for k in range(groups - 1, 0, -1):
        @pl.when(group + k < groups)
        def _(k=k):
            for copy in ahead_pair(k, group + k):
                copy.start()

    for b in range(count):
        coefs = [
            jnp.where(
                keys[o] < keys[b], jnp.exp(jnp.minimum(before[b] - upto[o], 0.0)), 0.0
            )
            for o in range(count)
            if o != b
        ]
        others = [o for o in range(count) if o != b]
        for i in range(share):
            span = slice(i * 64, (i + 1) * 64)
            acc = jnp.zeros((64, 128), F32)
            for o, coef in zip(others, coefs):
                acc = acc + coef[i : i + 1, :] * got_s[o, span, :].astype(F32)
            within_s[b, span, :] = acc

    inside_span(1)
    carry = within_s.at[count]
    carry[...] = jnp.zeros((rows, 128), F32)
    for k in range(groups - 1, 0, -1):
        @pl.when(group - k >= 0)
        def _(k=k):
            for copy in ahead_pair(k, group - k):
                copy.wait_recv()
            decay = jnp.exp(aggnotes_s[k])
            for i in range(share):
                span = slice(i * 64, (i + 1) * 64)
                carry[span, :] = decay[i : i + 1, :] * carry[span, :] + aggs_s[k, span, :].astype(F32)

    def entering(q):
        factor = before_s[q]
        parts = []
        for i in range(share):
            span = slice(i * 64, (i + 1) * 64)
            parts.append(factor[i : i + 1, :] * carry[span, :] + within_s[q, span, :])
        return jnp.concatenate(parts, axis=0).astype(BF16)

    for d in range(1, count):
        q = lax.rem(me + d, count)
        send_s[d] = entering(q)
        sends.append(exchange(send_s.at[d], ent_s.at[me], sem_c, d, q))
        sends[-1].start()
    ent_s[me] = entering(me)
    inside_span(2)
    for d in range(1, count):
        src = lax.rem(me - d + count, count)
        exchange(send_s.at[d], ent_s.at[src], sem_c, d, src).wait_recv()
    tokens, width = inside_s.shape
    width_out = w_s.shape[1]
    piece = mine_s.shape[1]
    chunk = max(piece, TILE)
    chunks = tokens // chunk
    per_chunk = chunk // piece
    shift = (1 - band // (bands // 2)) * (chunks // 2)

    def chunk_of(i):
        return lax.rem(shift + i, chunks)

    def rows_of(i):
        return pl.ds(pl.multiple_of(chunk_of(i) * chunk, chunk), chunk)

    def to(j):
        return {"seq": j, "view": view}

    @pl.loop(0, pairs)
    def _(pair):
        rows = pl.ds(pl.multiple_of(pair * 128, 128), 128)
        per = share // 2
        mine = ent_s[pair // per, pl.ds(pl.multiple_of(lax.rem(pair, per) * 128, 128), 128), :]
        entry_s[0, rows, :] = mine
        before = jnp.ones((128, 128), F32)
        for c in range(1, spans):
            e0, e1 = pair_columns(ecol_s[c * GROUP - 8 : c * GROUP, :], pair)
            before = before * jnp.where(top_half, e0[7:8, :], e1[7:8, :])
            entry = before * mine.astype(F32) + prefix_ref[c - 1, rows, :]
            entry_s[c, rows, :] = entry.astype(BF16)

    load_gate.wait()
    def send(j):
        return pltpu.make_async_remote_copy(
            src_ref=mine_s.at[j], dst_ref=out_hbm.at[band],
            send_sem=sem.at[0, j], recv_sem=sem.at[1, band],
            device_id=to(j), device_id_type=MESH,
        )

    def arrival(i):
        return pltpu.make_async_remote_copy(
            src_ref=mine_s.at[i], dst_ref=out_hbm.at[i],
            send_sem=sem.at[0, i], recv_sem=sem.at[1, i],
            device_id=to(i), device_id_type=MESH,
        )

    half = iota((chunk, 128), 1) < 64
    same = (iota((128, 128), 0) < 64) == (iota((128, 128), 1) < 64)
    block = jnp.where(same, 1.0 / 64.0, 0.0).astype(BF16)
    for i in range(chunks):
        rows = rows_of(i)
        part = chunk_of(i) * chunk // GROUP
        def one(pair):
            lanes = pl.ds(pl.multiple_of(pair * 128, 128), 128)
            e0, e1 = pair_columns(ecol_s[rows, :], pair)
            carried = nt(c_ref[rows, :], entry_s[part, lanes, :])
            carried = carried * jnp.where(half, e0, e1)
            gate = gate_s[rows, lanes].astype(F32)
            g = (inside_s[rows, lanes] + carried) * (gate / (1.0 + jnp.exp(-gate)))
            square = g * g
            high = square.astype(BF16)
            low = (square - high.astype(F32)).astype(BF16)
            mean = nn(high, block) + nn(low, block)
            normed = g * lax.rsqrt(mean + EPS) * gain_ref[:, lanes]
            normed_s[:, lanes] = normed.astype(BF16)

        @pl.loop(0, pairs // 4)
        def _(quad):
            for k in range(4):
                one(quad * 4 + k)

        if i == 0:
            load_w.wait()
        base = chunk_of(i) * per_chunk

        @pl.loop(0, width_out // 256)
        def _(n):
            cols = pl.ds(pl.multiple_of(n * 256, 256), 256)
            made = nn(normed_s[...], w_s[:, cols])
            for u in range(per_chunk):
                mine_s[base + u, :, cols] = made[u * piece : (u + 1) * piece, :].astype(BF16)

        for u in range(per_chunk):
            j = base + u

            @pl.when(j != band)
            def _(j=j):
                send(j).start()

    keep = pltpu.make_async_copy(mine_s.at[band], out_hbm.at[band], sem_o)
    keep.start()
    for d in range(1, bands):
        arrival(lax.rem(band - d + bands, bands)).wait_recv()
    for copy in sends:
        copy.wait_send()
    for step in range(1, groups):
        @pl.when(group + step < groups)
        def _(step=step):
            for copy in ahead_pair(step, group + step):
                copy.wait_send()
    for d in range(1, bands):
        send(lax.rem(band + d, bands)).wait_send()
    keep.wait()


def mixer_part(order, skip, b, c, ld, gain, x, gate, w, views, bands):
    heads, tokens = ld.shape
    width, width_out = w.shape
    pack = 2 if bands % 2 == 0 and heads % (4 * views) == 0 else 1
    count = views * pack
    share = heads // count
    groups = bands // pack
    rows = share * 64
    piece = tokens // bands
    spans = tokens // GROUP
    vmem = pl.BlockSpec(memory_space=pltpu.VMEM)
    hbm = pl.BlockSpec(memory_space=pl.ANY)
    smem = pl.BlockSpec(memory_space=pltpu.SMEM)
    dma = pltpu.SemaphoreType.DMA
    sems = lambda n: dma((2, n))
    return pl.pallas_call(
        functools.partial(mixer_kernel, views, pack, groups, share, bands),
        in_specs=[smem] * 2 + [vmem] * 4 + [hbm] * 3,
        out_specs=hbm,
        out_shape=jax.ShapeDtypeStruct((bands, piece, width_out), BF16),
        scratch_shapes=[
            VMEM(x.shape, BF16),
            VMEM(x.shape, F32),
            VMEM(x.shape, BF16),
            VMEM(w.shape, BF16),
            dma, dma, dma, dma,
            VMEM((tokens, 128), F32),
            VMEM((heads, tokens), F32),
            VMEM((spans, GROUP, GROUP), F32),
            VMEM((tokens, 128), F32),
            VMEM((heads, 128), F32),
            VMEM((count, rows, 128), BF16),
            VMEM((spans - 1, width, 128), F32),
            VMEM((count, rows, 128), BF16),
            VMEM((count, 8, 128), F32),
            VMEM((count, rows, 128), BF16),
            VMEM((count, 8, 128), F32),
            VMEM((rows, 128), BF16),
            VMEM((8, 128), F32),
            VMEM((groups, rows, 128), BF16),
            VMEM((groups, 8, 128), F32),
            VMEM((count + 1, rows, 128), F32),
            VMEM((count, 8, 128), F32),
            VMEM((count, rows, 128), BF16),
            sems(count), sems(count), sems(groups), sems(groups), sems(count),
            VMEM((tokens, 128), F32),
            VMEM((spans, width, 128), BF16),
            VMEM((max(piece, TILE), width), BF16),
            VMEM((bands, piece, width_out), BF16),
            sems(bands),
        ],
        compiler_params=pltpu.CompilerParams(
            collective_id=0, has_side_effects=True, vmem_limit_bytes=VMEM_LIMIT
        ),
        name="mixer_part",
    )(order, skip, b, c, ld, gain, x, gate, w)


def tile_kernel(order_ref, in_ref, out_ref):
    out_ref[...] = in_ref[...]


def tile_part(order, pieces):
    bands, piece, width = pieces.shape
    per = TILE // piece
    block = (per, piece, width)
    return pl.pallas_call(
        tile_kernel,
        grid_spec=pltpu.PrefetchScalarGridSpec(
            num_scalar_prefetch=1,
            grid=(bands // per,),
            in_specs=[pl.BlockSpec(block, lambda k, order: (order[k], 0, 0))],
            out_specs=pl.BlockSpec(block, lambda k, order: (k, 0, 0)),
        ),
        out_shape=jax.ShapeDtypeStruct(pieces.shape, BF16),
        compiler_params=pltpu.CompilerParams(vmem_limit_bytes=VMEM_LIMIT),
        name="tile_part",
    )(order, pieces)


def shards(
    ssd_input, gate_input, b_matrix, c_matrix, log_decay,
    d_skip, norm_gain, out_weight, view_order, tile_order,
):
    views, bands = lax.axis_size("view"), lax.axis_size("seq")
    x, gate = ssd_input[0, 0], gate_input[0, 0]
    b, c, ld = b_matrix[0, 0], c_matrix[0, 0], log_decay[0, 0]
    tokens, width = x.shape
    pieces = mixer_part(
        view_order, d_skip, b, c, ld, norm_gain[None, :], x, gate, out_weight, views, bands
    )
    out = tile_part(tile_order[0], pieces)
    return out.reshape(1, 1, tokens, out_weight.shape[1])


def solution(mesh):
    whole = P("seq", "view", None, None)
    in_specs = (whole,) * 5 + (P(), P(), P(), P("seq", None), P("seq", None))
    return jax.shard_map(
        shards, mesh=mesh, in_specs=in_specs, out_specs=whole, check_vma=False
    )
```

time: 87.9 us -> 77.2 us (0.88)
  the two profiles are of different devices: /device:TPU:29 before, /device:TPU:13 now
where the time goes in v3:
time: 77.2 us; the launch traced here: 77 us
  Pallas kernels  77 us (100%)
    pallas_call x1, Pallas kernels, mixer_part(): pl.pallas_call(functools.partial(mixer_kernel, views, pack, groups, share...  72.7 us
    pallas_call x1, Pallas kernels, tile_part(): pl.pallas_call(tile_kernel, grid_spec=pltpu.PrefetchScalarGridSpec(num_sc...  4.24 us

profile of v3, /device:TPU:13, one launch (start us, length us, event | category | flops | bytes accessed | tf_op | source)
XLA Modules:
  0.0 77.0 jit_solution(5865204525412472851)
XLA Ops:
  0.0 72.7 %mixer_part.1.in_ref = bf16[8,64,1536]{2,1,0:T(8,128)(2,1)} custom-call(s32[1,4]{1,0:T(1,128)} %order_ref.1, f32[32]{0:T(128)} %skip_ref.1, bf16[512,128]{1,0:T(8,128)(2,1)} %bitcast.10, bf16[512,128]{1,0:T(8,128)(2,1)} %bitcast.11, f32[32,512]{1,0:T(8,128)} %bitcast.12, f32[1,2048]{1,0:T(1,128)} %bitcast.13, bf16[512,2048]{1,0:T(8,128)(2,1)} %bitcast.8, ...), custom_call_target="tpu_custom_call" | custom-call | tf_op jit(solution)/shard_map/mixer_part/pallas_call | solution.py:397
  72.7 4.2 %tile_part.1 = bf16[8,64,1536]{2,1,0:T(8,128)(2,1)} custom-call(s32[4]{0:T(128)} %bitcast.14, bf16[8,64,1536]{2,1,0:T(8,128)(2,1)} %mixer_part.1.in_ref), custom_call_target="tpu_custom_call" | custom-call | tf_op jit(solution)/shard_map/tile_part/pallas_call | solution.py:448
